TPU v7x, 256 devices: a whole 4x4x8 slice. The times are simulated.
256 devices in a mesh: section: 4 (over x), dom: 64 (over y, z, core).
Axes of the slice: x: 4, y: 4, z: 8, core: 2. Of those that a mesh axis runs over, the one named last changes fastest.
Arguments:
- layer_inputs: bfloat16 [4, 1, 24576, 512], P('section', None, 'dom'), may hold values from -6 to 6
- top_grad: bfloat16 [1, 24576, 512], P(None, 'dom'), may hold values from -6 to 6
- w_qkv: bfloat16 [4, 512, 1536], P('section')
- w_out: bfloat16 [4, 512, 512], P('section'), may hold values from -0.25 to 0.25
- neighbours: int32 [192, 3], P('dom'), may hold values from -1 to 191, as said below
Outputs:
- input_grads: bfloat16 [4, 1, 24576, 512], P('section', None, 'dom')
- qkv_grad: float32 [4, 512, 1536], P('section', 'dom')
- out_grad: float32 [4, 512, 512], P('section', 'dom')
Inputs may be any that keep to these rules, and one draw needn't show every extreme that they name: `neighbours`: entry 0 of block b is b; the other entries name distinct blocks (b + o) mod 192 with 0 < |o| <= 1, then -1 to the end of the row. The first block of every index of dom lists 3 blocks.
All inputs are finite; a program needn't handle non-finite values.
Results may differ from a plain program's by a relative error of at most 0.017.
Values may be sent and summed in bfloat16 or wider, within the bound.
A program may use at most 128 MiB of HBM per device.

v0:
```python
import jax
import jax.numpy as jnp
from jax import lax
from jax.sharding import PartitionSpec as P

HEADS = 8
KMAX = 3
HALO = 1


def extended_2(block, sides, width):
    for axis, dim in sides:
        count = lax.axis_size(axis)
        forward = [(i, i + 1) for i in range(count - 1)]
        forward.append((count - 1, 0))
        backward = [(target, source) for source, target in forward]
        low = lax.ppermute(
            lax.slice_in_dim(block, block.shape[dim] - width, None, axis=dim), axis, forward
        )
        high = lax.ppermute(lax.slice_in_dim(block, 0, width, axis=dim), axis, backward)
        block = jnp.concatenate([low, block, high], axis=dim)
    return block


def shifted(block, axis, distance):
    devices = range(lax.axis_size(axis))
    route = [((i - distance) % len(devices), i) for i in devices]
    return lax.ppermute(block, axis, route)


def shifted_2(block, axis, distance):
    devices = range(lax.axis_size(axis))
    route = [(i - distance, i) for i in devices if i - distance in devices]
    return lax.ppermute(block, axis, route)


def fetch_rims(keyval):
    extended = extended_2(keyval, (("dom", 0),), HALO)
    return extended


def layer_back(x, g, w_qkv, w_out, neighbours):
    blk, tile, width = x.shape
    hdim = width // HEADS
    scale = 1.0 / hdim**0.5
    xf = x.astype(jnp.float32)
    mean_value = jnp.mean(xf, axis=-1, keepdims=True)
    centered_input = xf - mean_value
    inverse_deviation = lax.rsqrt(
        jnp.mean(centered_input * centered_input, axis=-1, keepdims=True) + 1e-05
    )
    normalized_input = centered_input * inverse_deviation
    normed_rows = normalized_input.astype(jnp.bfloat16)
    flat = normed_rows.reshape(blk * tile, width)
    qkv = jnp.dot(flat, w_qkv, preferred_element_type=jnp.float32).astype(jnp.bfloat16)
    qkv = qkv.reshape(blk, tile, 3 * width)
    query = qkv[..., :width].reshape(blk, tile, HEADS, hdim)
    extended = fetch_rims(qkv[..., width:])
    parts = lax.axis_size("dom")
    where_me = lax.axis_index("dom")
    valid = neighbours >= 0
    where_at = jnp.where(valid, (neighbours - where_me * blk + HALO) % (blk * parts), 0)
    tiles = extended[where_at]
    keys = tiles[..., :width].reshape(blk, KMAX * tile, HEADS, hdim)
    values = tiles[..., width:].reshape(blk, KMAX * tile, HEADS, hdim)
    mask = jnp.repeat(valid, tile, axis=1)[:, None, None, :]
    scores = jnp.einsum("bqhd,bkhd->bhqk", query, keys, preferred_element_type=jnp.float32) * scale
    scores = jnp.where(mask, scores, -1e30)
    top = jnp.max(scores, axis=-1, keepdims=True)
    expo = jnp.exp(scores - top)
    probs = expo / jnp.sum(expo, axis=-1, keepdims=True)
    probs_b = probs.astype(jnp.bfloat16)
    attn = jnp.einsum(
        "bhqk,bkhd->bqhd", probs_b, values, preferred_element_type=jnp.float32
    ).astype(jnp.bfloat16)
    attn = attn.reshape(blk * tile, width)
    grad_rows = g.reshape(blk * tile, width)
    d_attn = jnp.dot(grad_rows, w_out.T, preferred_element_type=jnp.float32).astype(jnp.bfloat16)
    d_attn = d_attn.reshape(blk, tile, HEADS, hdim)
    d_prob = jnp.einsum("bqhd,bkhd->bhqk", d_attn, values, preferred_element_type=jnp.float32)
    d_score = (probs * (d_prob - jnp.sum(d_prob * probs, axis=-1, keepdims=True)) * scale).astype(
        jnp.bfloat16
    )
    d_query = jnp.einsum("bhqk,bkhd->bqhd", d_score, keys, preferred_element_type=jnp.float32)
    d_keys = jnp.einsum("bhqk,bqhd->bkhd", d_score, query, preferred_element_type=jnp.float32)
    d_values = jnp.einsum("bhqk,bqhd->bkhd", probs_b, d_attn, preferred_element_type=jnp.float32)
    d_tiles = jnp.concatenate(
        [d_keys.reshape(blk, KMAX, tile, width), d_values.reshape(blk, KMAX, tile, width)], axis=-1
    )
    slots = blk + 2 * HALO
    weighted = d_tiles * valid[:, :, None, None].astype(jnp.float32)
    d_extended = jnp.zeros((slots, tile, 2 * width), jnp.float32)
    d_extended = d_extended.at[where_at.reshape(-1)].add(
        weighted.reshape(blk * KMAX, tile, 2 * width)
    )
    lower_rim = d_extended[:HALO].astype(jnp.bfloat16)
    upper_rim = d_extended[HALO + blk :].astype(jnp.bfloat16)
    from_next = shifted(lower_rim, "dom", -1)
    from_prev = shifted(upper_rim, "dom", 1)
    d_keyval = d_extended[HALO : HALO + blk]
    d_keyval = d_keyval.at[blk - HALO :].add(from_next.astype(jnp.float32))
    d_keyval = d_keyval.at[:HALO].add(from_prev.astype(jnp.float32))
    d_qkv = jnp.concatenate([d_query.reshape(blk, tile, width), d_keyval], axis=-1).astype(
        jnp.bfloat16
    )
    d_qkv = d_qkv.reshape(blk * tile, 3 * width)
    normed_gradient = jnp.dot(d_qkv, w_qkv.T, preferred_element_type=jnp.float32).reshape(
        blk, tile, width
    )
    layernorm_gradient = inverse_deviation * (
        normed_gradient
        - jnp.mean(normed_gradient, axis=-1, keepdims=True)
        - normalized_input * jnp.mean(normed_gradient * normalized_input, axis=-1, keepdims=True)
    )
    d_input = (g.astype(jnp.float32) + layernorm_gradient).astype(jnp.bfloat16)
    return (d_input, flat, d_qkv, attn, grad_rows)


def local(layer_inputs, top_grad, w_qkv, w_out, neighbours):
    sections = lax.axis_size("section")
    section_me = lax.axis_index("section")
    micro = top_grad.shape[0]
    rows = top_grad.shape[1]
    width = top_grad.shape[2]
    blk = neighbours.shape[0]
    tile = rows // blk
    weight_in = w_qkv[0]
    weight_out = w_out[0]
    saved = layer_inputs[0]
    ticks = micro + sections - 1
    extra = (jnp.zeros((width, 3 * width), jnp.float32), jnp.zeros((width, width), jnp.float32))
    start_carry = (
        jnp.zeros((rows, width), jnp.bfloat16),
        jnp.zeros((micro, rows, width), jnp.bfloat16),
        extra,
    )

    def advance(tick, carry):
        received, results, extra = carry
        micro_idx = tick - (sections - 1 - section_me)
        active = (micro_idx >= 0) & (micro_idx < micro)
        safe = jnp.clip(micro_idx, 0, micro - 1)
        x_now = lax.dynamic_index_in_dim(saved, safe, 0, keepdims=False).reshape(blk, tile, width)
        top_now = lax.dynamic_index_in_dim(top_grad, safe, 0, keepdims=False)
        g_now = jnp.where(section_me == sections - 1, top_now, received).reshape(blk, tile, width)
        d_input, flat, d_qkv, attn, grad_rows = layer_back(
            x_now, g_now, weight_in, weight_out, neighbours
        )
        d_rows = d_input.reshape(rows, width)
        results = jnp.where(
            active, lax.dynamic_update_index_in_dim(results, d_rows, safe, 0), results
        )
        qkv_term = jnp.einsum("rd,re->de", flat, d_qkv, preferred_element_type=jnp.float32)
        out_term = jnp.einsum("rd,re->de", attn, grad_rows, preferred_element_type=jnp.float32)
        extra = (
            extra[0] + jnp.where(active, qkv_term, 0.0),
            extra[1] + jnp.where(active, out_term, 0.0),
        )
        received = shifted_2(d_rows, "section", -1)
        return (received, results, extra)

    received, results, extra = lax.fori_loop(0, ticks, advance, start_carry)
    first_part = extra[0]
    second_part = extra[1]
    summed = lax.psum_scatter(
        jnp.concatenate([first_part, second_part], axis=-1), "dom", scatter_dimension=0, tiled=True
    )
    return (results[None], summed[None, :, : 3 * width], summed[None, :, 3 * width :])


def solution(mesh):
    placed = (
        P("section", None, "dom", None),
        P(None, "dom", None),
        P("section", None, None),
        P("section", None, None),
        P("dom", None),
    )
    return jax.shard_map(
        local,
        mesh=mesh,
        in_specs=placed,
        out_specs=(
            P("section", None, "dom", None),
            P("section", "dom", None),
            P("section", "dom", None),
        ),
        check_vma=False,
    )
```

profile of v0, /device:TPU:1, one launch (start us, length us, event | category | flops | bytes accessed | tf_op | source)
XLA Modules:
  0.0 748.9 jit_solution(7500813417961625853)
XLA Ops:
  32.8 559.1 %while.25 = (s32[]{:T(128)}, bf16[384,512]{1,0:T(8,128)(2,1)S(1)}, bf16[1,384,512]{2,1,0:T(8,128)(2,1)}, f32[512,1536]{1,0:T(8,128)}, f32[512,512]{1,0:T(8,128)}...) while((s32[]{:T(128)}, bf16[384,512]{1,0:T(8,128)(2,1)S(1)}, ...), condition=%wide.region_11.12_spmd.clone, body=%wide.region_3.11_spmd.clone.sunk | while | flops 3188003072 | bytes 227787952 | solution.py:162
  60.5 25.4 %fusion.148 = f32[3,384,8,64]{1,3,2,0:T(8,128)} fusion(bf16[3,128,8,64]{1,3,2,0:T(8,128)(2,1)} %bitcast.180, f32[3,8,128,384]{3,2,1,0:T(8,128)} %fusion.147, f32[3,8,128,384]{3,2,1,0:T(8,128)} %copy-done.23, f32[3,8,128]{2,1,0:T(8,128)} %copy-done.24, f32[3,8,128]{2,1,0:T(8,128)} %get-tuple-element.662, pred[3,384]{1,0:T(4,128)(4,1)} %bitcast.189), kind=kOutput, calls=%fused_computation.19.clone.1 | convolution fusion | flops 166333824 | bytes 12215424 | tf_op jit(solution)/shard_map/while/body/eval_jaxpr/bhqk,bqhd->bkhd/dot_general | solution.py:85
  93.0 5.0 copy.53
  107.9 7.7 %scatter_fusion = f32[5,128,1024]{2,1,0:T(8,128)S(1)} fusion(f32[5,128,1024]{2,1,0:T(8,128)S(1)} %broadcast.703, s32[9]{0:T(128)S(1)} %fusion.144, f32[9,128,1024]{2,1,0:T(8,128)} %maximum_multiply_fusion.2), kind=kCustom, calls=%fused_computation.1.clone.clone.1 | custom fusion | flops 1179648 | bytes 14155812 | tf_op jit(solution)/shard_map/while/body/eval_jaxpr/scatter-add | solution.py:93
  130.6 22.5 %fusion.152 = bf16[3,8,128,64]{2,3,1,0:T(8,128)(2,1)} fusion(bf16[3,384,8,64]{1,3,2,0:T(8,128)(2,1)} %reshape.605, f32[3,8,128,384]{3,2,1,0:T(8,128)} %fusion.147, f32[3,8,128,384]{3,2,1,0:T(8,128)} %copy-done.23, f32[3,8,128]{2,1,0:T(8,128)S(1)} %copy-done.25, f32[3,8,128]{2,1,0:T(8,128)S(1)} %copy-done.21, pred[3,384]{1,0:T(4,128)(4,1)S(1)} %bitcast.193), kind=kOutput, calls=%fused_computation.24.clone.1 | convolution fusion | flops 166530432 | bytes 11035776 | tf_op jit(solution)/shard_map/while/body/eval_jaxpr/bhqk,bkhd->bqhd/dot_general | solution.py:84
  166.3 5.5 collective-permute-done.2
  199.3 25.4 %fusion.148 = f32[3,384,8,64]{1,3,2,0:T(8,128)} fusion(bf16[3,128,8,64]{1,3,2,0:T(8,128)(2,1)} %bitcast.180, f32[3,8,128,384]{3,2,1,0:T(8,128)} %fusion.147, f32[3,8,128,384]{3,2,1,0:T(8,128)} %copy-done.23, f32[3,8,128]{2,1,0:T(8,128)} %copy-done.24, f32[3,8,128]{2,1,0:T(8,128)} %get-tuple-element.662, pred[3,384]{1,0:T(4,128)(4,1)} %bitcast.189), kind=kOutput, calls=%fused_computation.19.clone.1 | convolution fusion | flops 166333824 | bytes 12215424 | tf_op jit(solution)/shard_map/while/body/eval_jaxpr/bhqk,bqhd->bkhd/dot_general | solution.py:85
  231.7 5.0 copy.53
  246.7 7.7 %scatter_fusion = f32[5,128,1024]{2,1,0:T(8,128)S(1)} fusion(f32[5,128,1024]{2,1,0:T(8,128)S(1)} %broadcast.703, s32[9]{0:T(128)S(1)} %fusion.144, f32[9,128,1024]{2,1,0:T(8,128)} %maximum_multiply_fusion.2), kind=kCustom, calls=%fused_computation.1.clone.clone.1 | custom fusion | flops 1179648 | bytes 14155812 | tf_op jit(solution)/shard_map/while/body/eval_jaxpr/scatter-add | solution.py:93
  255.5 6.3 collective-permute-start
  271.4 22.5 %fusion.152 = bf16[3,8,128,64]{2,3,1,0:T(8,128)(2,1)} fusion(bf16[3,384,8,64]{1,3,2,0:T(8,128)(2,1)} %reshape.605, f32[3,8,128,384]{3,2,1,0:T(8,128)} %fusion.147, f32[3,8,128,384]{3,2,1,0:T(8,128)} %copy-done.23, f32[3,8,128]{2,1,0:T(8,128)S(1)} %copy-done.25, f32[3,8,128]{2,1,0:T(8,128)S(1)} %copy-done.21, pred[3,384]{1,0:T(4,128)(4,1)S(1)} %bitcast.193), kind=kOutput, calls=%fused_computation.24.clone.1 | convolution fusion | flops 166530432 | bytes 11035776 | tf_op jit(solution)/shard_map/while/body/eval_jaxpr/bhqk,bkhd->bqhd/dot_general | solution.py:84
  307.1 5.5 collective-permute-done.2
  340.1 25.4 %fusion.148 = f32[3,384,8,64]{1,3,2,0:T(8,128)} fusion(bf16[3,128,8,64]{1,3,2,0:T(8,128)(2,1)} %bitcast.180, f32[3,8,128,384]{3,2,1,0:T(8,128)} %fusion.147, f32[3,8,128,384]{3,2,1,0:T(8,128)} %copy-done.23, f32[3,8,128]{2,1,0:T(8,128)} %copy-done.24, f32[3,8,128]{2,1,0:T(8,128)} %get-tuple-element.662, pred[3,384]{1,0:T(4,128)(4,1)} %bitcast.189), kind=kOutput, calls=%fused_computation.19.clone.1 | convolution fusion | flops 166333824 | bytes 12215424 | tf_op jit(solution)/shard_map/while/body/eval_jaxpr/bhqk,bqhd->bkhd/dot_general | solution.py:85
  372.5 5.0 copy.53
  387.5 7.7 %scatter_fusion = f32[5,128,1024]{2,1,0:T(8,128)S(1)} fusion(f32[5,128,1024]{2,1,0:T(8,128)S(1)} %broadcast.703, s32[9]{0:T(128)S(1)} %fusion.144, f32[9,128,1024]{2,1,0:T(8,128)} %maximum_multiply_fusion.2), kind=kCustom, calls=%fused_computation.1.clone.clone.1 | custom fusion | flops 1179648 | bytes 14155812 | tf_op jit(solution)/shard_map/while/body/eval_jaxpr/scatter-add | solution.py:93
  396.3 5.1 collective-permute-start
  411.1 22.5 %fusion.152 = bf16[3,8,128,64]{2,3,1,0:T(8,128)(2,1)} fusion(bf16[3,384,8,64]{1,3,2,0:T(8,128)(2,1)} %reshape.605, f32[3,8,128,384]{3,2,1,0:T(8,128)} %fusion.147, f32[3,8,128,384]{3,2,1,0:T(8,128)} %copy-done.23, f32[3,8,128]{2,1,0:T(8,128)S(1)} %copy-done.25, f32[3,8,128]{2,1,0:T(8,128)S(1)} %copy-done.21, pred[3,384]{1,0:T(4,128)(4,1)S(1)} %bitcast.193), kind=kOutput, calls=%fused_computation.24.clone.1 | convolution fusion | flops 166530432 | bytes 11035776 | tf_op jit(solution)/shard_map/while/body/eval_jaxpr/bhqk,bkhd->bqhd/dot_general | solution.py:84
  446.8 5.5 collective-permute-done.2
  479.8 25.4 %fusion.148 = f32[3,384,8,64]{1,3,2,0:T(8,128)} fusion(bf16[3,128,8,64]{1,3,2,0:T(8,128)(2,1)} %bitcast.180, f32[3,8,128,384]{3,2,1,0:T(8,128)} %fusion.147, f32[3,8,128,384]{3,2,1,0:T(8,128)} %copy-done.23, f32[3,8,128]{2,1,0:T(8,128)} %copy-done.24, f32[3,8,128]{2,1,0:T(8,128)} %get-tuple-element.662, pred[3,384]{1,0:T(4,128)(4,1)} %bitcast.189), kind=kOutput, calls=%fused_computation.19.clone.1 | convolution fusion | flops 166333824 | bytes 12215424 | tf_op jit(solution)/shard_map/while/body/eval_jaxpr/bhqk,bqhd->bkhd/dot_general | solution.py:85
  527.2 7.7 %scatter_fusion = f32[5,128,1024]{2,1,0:T(8,128)S(1)} fusion(f32[5,128,1024]{2,1,0:T(8,128)S(1)} %broadcast.703, s32[9]{0:T(128)S(1)} %fusion.144, f32[9,128,1024]{2,1,0:T(8,128)} %maximum_multiply_fusion.2), kind=kCustom, calls=%fused_computation.1.clone.clone.1 | custom fusion | flops 1179648 | bytes 14155812 | tf_op jit(solution)/shard_map/while/body/eval_jaxpr/scatter-add | solution.py:93
  536.0 5.1 collective-permute-start
  550.8 22.5 %fusion.152 = bf16[3,8,128,64]{2,3,1,0:T(8,128)(2,1)} fusion(bf16[3,384,8,64]{1,3,2,0:T(8,128)(2,1)} %reshape.605, f32[3,8,128,384]{3,2,1,0:T(8,128)} %fusion.147, f32[3,8,128,384]{3,2,1,0:T(8,128)} %copy-done.23, f32[3,8,128]{2,1,0:T(8,128)S(1)} %copy-done.25, f32[3,8,128]{2,1,0:T(8,128)S(1)} %copy-done.21, pred[3,384]{1,0:T(4,128)(4,1)S(1)} %bitcast.193), kind=kOutput, calls=%fused_computation.24.clone.1 | convolution fusion | flops 166530432 | bytes 11035776 | tf_op jit(solution)/shard_map/while/body/eval_jaxpr/bhqk,bkhd->bqhd/dot_general | solution.py:84
  586.5 5.5 collective-permute-done.2
  596.6 142.7 %reduce-scatter.2.cloned.1.call-done = f32[8,2048]{1,0:T(8,128)} async-done(((f32[512,2048]{1,0:T(8,128)}), f32[8,2048]{1,0:T(8,128)}) %reduce-scatter.2.cloned.1.call-update) | async-done | bytes 65552 | tf_op jit(solution)/shard_map/reduce_scatter | solution.py:165
  (417 shorter events, 314.2 us)
Async XLA Ops:
  7.2 732.1 %reduce-scatter.2.cloned.1.call-start = ((), (), s32[]{:S(2)}) async-start(), calls=%async_computation.1 | async-start | bytes 4259840 | tf_op jit(solution)/shard_map/reduce_scatter | solution.py:165
  12.1 6.4 collective-permute-start.3
  15.2 5.8 collective-permute-start.4
  116.7 39.6 %collective-permute-start = (bf16[1,128,1024]{2,1,0:T(8,128)(2,1)}, bf16[1,128,1024]{2,1,0:T(8,128)(2,1)}, u32[]{:S(2)}, u32[]{:S(2)}) collective-permute-start(bf16[1,128,1024]{2,1,0:T(8,128)(2,1)} %get-tuple-element.605), channel_id=1, source_target_pairs={{1,0},{2,1},{3,2},{4,3},{5,4},{6,5},{7,6},{8,7},{9,8},{10,9},{11,1... | collective-permute-start | bytes 786440 | tf_op jit(solution)/shard_map/while/body/eval_jaxpr/ppermute | solution.py:28
  121.2 37.0 %collective-permute-start.1 = (bf16[1,128,1024]{2,1,0:T(8,128)(2,1)}, bf16[1,128,1024]{2,1,0:T(8,128)(2,1)}, u32[]{:S(2)}, u32[]{:S(2)}) collective-permute-start(bf16[1,128,1024]{2,1,0:T(8,128)(2,1)} %get-tuple-element.606), channel_id=1, source_target_pairs={{63,0},{0,1},{1,2},{2,3},{3,4},{4,5},{5,6},{6,7},{7,8},{8,9},{9,10... | collective-permute-start | bytes 786440 | tf_op jit(solution)/shard_map/while/body/eval_jaxpr/ppermute | solution.py:28
  163.1 8.7 %collective-permute-start.2 = (bf16[384,512]{1,0:T(8,128)(2,1)S(1)}, bf16[384,512]{1,0:T(8,128)(2,1)S(1)}, u32[]{:S(2)}, u32[]{:S(2)}) collective-permute-start(bf16[384,512]{1,0:T(8,128)(2,1)S(1)} %bitcast.174), channel_id=1, source_target_pairs={{64,0},{128,64},{192,128},{65,1},{129,65},{193,129},{66,2},{130,66... | collective-permute-start | bytes 1179656 | tf_op jit(solution)/shard_map/while/body/eval_jaxpr/ppermute | solution.py:34
  164.7 7.0 copy-start.9
  164.7 7.0 copy-start.12
  254.4 7.3 copy-start.1
  254.4 7.3 copy-start.17
  254.4 7.3 copy-start.21
  254.4 7.3 copy-start.25
  255.5 41.7 %collective-permute-start = (bf16[1,128,1024]{2,1,0:T(8,128)(2,1)}, bf16[1,128,1024]{2,1,0:T(8,128)(2,1)}, u32[]{:S(2)}, u32[]{:S(2)}) collective-permute-start(bf16[1,128,1024]{2,1,0:T(8,128)(2,1)} %get-tuple-element.605), channel_id=1, source_target_pairs={{1,0},{2,1},{3,2},{4,3},{5,4},{6,5},{7,6},{8,7},{9,8},{10,9},{11,1... | collective-permute-start | bytes 786440 | tf_op jit(solution)/shard_map/while/body/eval_jaxpr/ppermute | solution.py:28
  261.7 37.4 %collective-permute-start.1 = (bf16[1,128,1024]{2,1,0:T(8,128)(2,1)}, bf16[1,128,1024]{2,1,0:T(8,128)(2,1)}, u32[]{:S(2)}, u32[]{:S(2)}) collective-permute-start(bf16[1,128,1024]{2,1,0:T(8,128)(2,1)} %get-tuple-element.606), channel_id=1, source_target_pairs={{63,0},{0,1},{1,2},{2,3},{3,4},{4,5},{5,6},{6,7},{7,8},{8,9},{9,10... | collective-permute-start | bytes 786440 | tf_op jit(solution)/shard_map/while/body/eval_jaxpr/ppermute | solution.py:28
  303.9 8.7 %collective-permute-start.2 = (bf16[384,512]{1,0:T(8,128)(2,1)S(1)}, bf16[384,512]{1,0:T(8,128)(2,1)S(1)}, u32[]{:S(2)}, u32[]{:S(2)}) collective-permute-start(bf16[384,512]{1,0:T(8,128)(2,1)S(1)} %bitcast.174), channel_id=1, source_target_pairs={{64,0},{128,64},{192,128},{65,1},{129,65},{193,129},{66,2},{130,66... | collective-permute-start | bytes 1179656 | tf_op jit(solution)/shard_map/while/body/eval_jaxpr/ppermute | solution.py:34
  305.5 7.0 copy-start.9
  396.3 40.5 %collective-permute-start = (bf16[1,128,1024]{2,1,0:T(8,128)(2,1)}, bf16[1,128,1024]{2,1,0:T(8,128)(2,1)}, u32[]{:S(2)}, u32[]{:S(2)}) collective-permute-start(bf16[1,128,1024]{2,1,0:T(8,128)(2,1)} %get-tuple-element.605), channel_id=1, source_target_pairs={{1,0},{2,1},{3,2},{4,3},{5,4},{6,5},{7,6},{8,7},{9,8},{10,9},{11,1... | collective-permute-start | bytes 786440 | tf_op jit(solution)/shard_map/while/body/eval_jaxpr/ppermute | solution.py:28
  401.4 37.4 %collective-permute-start.1 = (bf16[1,128,1024]{2,1,0:T(8,128)(2,1)}, bf16[1,128,1024]{2,1,0:T(8,128)(2,1)}, u32[]{:S(2)}, u32[]{:S(2)}) collective-permute-start(bf16[1,128,1024]{2,1,0:T(8,128)(2,1)} %get-tuple-element.606), channel_id=1, source_target_pairs={{63,0},{0,1},{1,2},{2,3},{3,4},{4,5},{5,6},{6,7},{7,8},{8,9},{9,10... | collective-permute-start | bytes 786440 | tf_op jit(solution)/shard_map/while/body/eval_jaxpr/ppermute | solution.py:28
  443.6 8.7 %collective-permute-start.2 = (bf16[384,512]{1,0:T(8,128)(2,1)S(1)}, bf16[384,512]{1,0:T(8,128)(2,1)S(1)}, u32[]{:S(2)}, u32[]{:S(2)}) collective-permute-start(bf16[384,512]{1,0:T(8,128)(2,1)S(1)} %bitcast.174), channel_id=1, source_target_pairs={{64,0},{128,64},{192,128},{65,1},{129,65},{193,129},{66,2},{130,66... | collective-permute-start | bytes 1179656 | tf_op jit(solution)/shard_map/while/body/eval_jaxpr/ppermute | solution.py:34
  445.2 7.0 copy-start.9
  536.0 40.5 %collective-permute-start = (bf16[1,128,1024]{2,1,0:T(8,128)(2,1)}, bf16[1,128,1024]{2,1,0:T(8,128)(2,1)}, u32[]{:S(2)}, u32[]{:S(2)}) collective-permute-start(bf16[1,128,1024]{2,1,0:T(8,128)(2,1)} %get-tuple-element.605), channel_id=1, source_target_pairs={{1,0},{2,1},{3,2},{4,3},{5,4},{6,5},{7,6},{8,7},{9,8},{10,9},{11,1... | collective-permute-start | bytes 786440 | tf_op jit(solution)/shard_map/while/body/eval_jaxpr/ppermute | solution.py:28
  541.1 37.4 %collective-permute-start.1 = (bf16[1,128,1024]{2,1,0:T(8,128)(2,1)}, bf16[1,128,1024]{2,1,0:T(8,128)(2,1)}, u32[]{:S(2)}, u32[]{:S(2)}) collective-permute-start(bf16[1,128,1024]{2,1,0:T(8,128)(2,1)} %get-tuple-element.606), channel_id=1, source_target_pairs={{63,0},{0,1},{1,2},{2,3},{3,4},{4,5},{5,6},{6,7},{7,8},{8,9},{9,10... | collective-permute-start | bytes 786440 | tf_op jit(solution)/shard_map/while/body/eval_jaxpr/ppermute | solution.py:28
  583.3 8.7 %collective-permute-start.2 = (bf16[384,512]{1,0:T(8,128)(2,1)S(1)}, bf16[384,512]{1,0:T(8,128)(2,1)S(1)}, u32[]{:S(2)}, u32[]{:S(2)}) collective-permute-start(bf16[384,512]{1,0:T(8,128)(2,1)S(1)} %bitcast.174), channel_id=1, source_target_pairs={{64,0},{128,64},{192,128},{65,1},{129,65},{193,129},{66,2},{130,66... | collective-permute-start | bytes 1179656 | tf_op jit(solution)/shard_map/while/body/eval_jaxpr/ppermute | solution.py:34
  584.9 7.0 copy-start.9
  (83 other events, 359.8 us)
Sparse Core Ops, SparseCore 0:
  596.7 142.5 reduce-scatter.1
where the time goes:
time: 757 us; the launch traced here: 749 us
  matrix products  279 us (37%)
  local copies, waits for them, and re-layouts  170 us (22%)
  waiting for transfers between devices  169 us (22%)
  other arithmetic  84.4 us (11%)
  starting transfers between devices  30.2 us (4%)
  between operations  14.2 us (2%)
    reduce_scatter x1, waiting for transfers between devices, local(): lax.psum_scatter(jnp.concatenate([first_part, second_part], axis=-1), 'do...  143 us
    dot_general x4, matrix products, layer_back(): jnp.einsum('bhqk,bqhd->bkhd', d_score, query, preferred_element_type=jnp....  102 us
    dot_general x4, matrix products, layer_back(): jnp.einsum('bhqk,bkhd->bqhd', d_score, keys, preferred_element_type=jnp.f...  90.1 us
    concatenate x8, local copies, waits for them, and re-layouts, layer_back(): jnp.concatenate([d_keys.reshape(blk, KMAX, tile, width), d_values.reshape...  34.1 us
    scatter-add x4, other arithmetic, layer_back(): d_extended.at[where_at.reshape(-1)]  30.9 us
    ppermute x4, waiting for transfers between devices, shifted_2(): return lax.ppermute(block, axis, route)  21.8 us
    ppermute x8, starting transfers between devices, shifted(): return lax.ppermute(block, axis, route)  21 us
    transpose x4, local copies, waits for them, and re-layouts, layer_back(): jnp.einsum('bhqk,bqhd->bkhd', d_score, query, preferred_element_type=jnp....  20 us
  transfers between devices with their start and end apart: 15, of which 7 were waited for; matrix products, arithmetic and copies ran while one was open for 21% of the time, Pallas kernels for 0%

commit v1 on v0

v1 whole, which is shorter than its diff:
```python
import jax
import jax.numpy as jnp
from jax import lax
from jax.experimental import pallas as pl
from jax.experimental.pallas import tpu as pltpu
from jax.sharding import PartitionSpec as P

SEC = 4
NY, NZ, NC = 4, 8, 2
DOM = NY * NZ * NC
D = 512
HEADS = 8
HDIM = D // HEADS
PAIRS = HEADS // 2
TILE = 128
BLK = 3
KEYS = 3 * TILE
ROWS = BLK * TILE
EXT = ROWS + 2 * TILE
COLS = 4
SCALE = 1.0 / HDIM**0.5
BF = jnp.bfloat16
F32 = jnp.float32
MESH = pl.DeviceIdType.MESH


def dot(a, b, ca, cb):
    return lax.dot_general(a, b, (((ca,), (cb,)), ((), ())), preferred_element_type=F32)


def body(
    nbr, x_hbm, g_hbm, wq_hbm, wo_hbm, gout_hbm, dwq_ref, dwo_ref,
    x_v, wq, wo, g_v, xhat, inv_v, xn, xnT, q2, kv, kT, pr, attnT, da2, acc,
    rim_lo, rim_hi, rim_next, rim_prev, dqkv, gout,
    gs, cs, cr, ys, yr, zs, zr,
    in_sem, out_sem, halo_s, halo_r, rim_s, rim_r, g_s, g_r,
    cs_s, cs_r, y_s, y_r, z_s, z_r,
):
    sec = lax.axis_index("section")
    dom = lax.axis_index("dom")
    y = lax.div(dom, NZ * NC)
    z = lax.rem(lax.div(dom, NC), NZ)
    c = lax.rem(dom, NC)
    nxt = lax.rem(dom + 1, DOM)
    prv = lax.rem(dom + DOM - 1, DOM)
    partner = dom + 1 - 2 * c
    before = lax.rem(sec + SEC - 1, SEC)
    after = lax.rem(sec + 1, SEC)

    def y_dev(o):
        return lax.rem(y + o, NY) * (NZ * NC) + z * NC + c

    def z_dev(o):
        return y * (NZ * NC) + lax.rem(z + o, NZ) * NC + c

    load_x = pltpu.make_async_copy(x_hbm, x_v, in_sem.at[0])
    load_wq = pltpu.make_async_copy(wq_hbm, wq, in_sem.at[1])
    load_wo = pltpu.make_async_copy(wo_hbm, wo, in_sem.at[2])
    load_g = pltpu.make_async_copy(g_hbm, g_v, in_sem.at[3])
    load_x.start()
    load_wq.start()
    load_wo.start()

    @pl.when(sec == SEC - 1)
    def _():
        load_g.start()

    barrier = pltpu.get_barrier_semaphore()
    peers = [(sec, nxt), (sec, prv), (sec, partner), (before, dom), (after, dom)]
    peers += [(sec, y_dev(o)) for o in range(1, NY)]
    peers += [(sec, z_dev(o)) for o in range(1, NZ)]
    for peer in peers:
        pl.semaphore_signal(barrier, inc=1, device_id=peer, device_id_type=MESH)

    lane = lax.broadcasted_iota(jnp.int32, (1, TILE), 1)
    m0 = jnp.where(lane < HDIM, 1.0, 0.0)
    m1 = 1.0 - m0

    load_x.wait()
    for b in range(BLK):
        rows = pl.ds(b * TILE, TILE)
        xf = x_v[rows, :].astype(F32)
        cen = xf - jnp.mean(xf, axis=-1, keepdims=True)
        inv = lax.rsqrt(jnp.mean(cen * cen, axis=-1, keepdims=True) + 1e-05)
        xh = cen * inv
        xhat[rows, :] = xh
        inv_v[rows, :] = jnp.broadcast_to(inv, (TILE, TILE))
        xn[rows, :] = xh.astype(BF)

    load_wq.wait()
    for h in range(2):
        part = dot(xn[...], wq[:, (1 + h) * D : (2 + h) * D], 1, 0)
        kv[TILE : TILE + ROWS, h * D : (h + 1) * D] = part.astype(BF)
    pl.semaphore_wait(barrier, len(peers))
    halo_up = pltpu.make_async_remote_copy(
        kv.at[pl.ds(ROWS, TILE)], kv.at[pl.ds(0, TILE)], halo_s.at[0], halo_r.at[0],
        device_id=(sec, nxt), device_id_type=MESH,
    )
    halo_dn = pltpu.make_async_remote_copy(
        kv.at[pl.ds(TILE, TILE)], kv.at[pl.ds(TILE + ROWS, TILE)], halo_s.at[1], halo_r.at[1],
        device_id=(sec, prv), device_id_type=MESH,
    )
    halo_up.start()
    halo_dn.start()

    qs = dot(xn[...], wq[:, 0:D], 1, 0).astype(BF).astype(F32) * SCALE
    for b in range(BLK):
        for p in range(PAIRS):
            qb = qs[b * TILE : (b + 1) * TILE, p * TILE : (p + 1) * TILE]
            q2[b * PAIRS + p, 0:TILE, :] = (qb * m0).astype(BF)
            q2[b * PAIRS + p, TILE:, :] = (qb * m1).astype(BF)

    def forward(b):
        here = dom * BLK + b
        low = lax.rem(here + DOM * BLK - 1, DOM * BLK)
        high = lax.rem(here + 1, DOM * BLK)
        n1 = jnp.full((TILE, 2 * TILE), nbr[b, 1], jnp.int32)
        n2 = jnp.full((TILE, 2 * TILE), nbr[b, 2], jnp.int32)
        has_low = (n1 == low) | (n2 == low)
        has_high = (n1 == high) | (n2 == high)
        for p in range(PAIRS):
            keys = kv[b * TILE : b * TILE + KEYS, p * TILE : (p + 1) * TILE]
            vals = kv[b * TILE : b * TILE + KEYS, D + p * TILE : D + (p + 1) * TILE]
            s = dot(keys, q2[b * PAIRS + p], 1, 1)
            s = jnp.concatenate(
                [
                    jnp.where(has_low, s[0:TILE], -1e30),
                    s[TILE : 2 * TILE],
                    jnp.where(has_high, s[2 * TILE :], -1e30),
                ],
                axis=0,
            )
            top = jnp.max(s, axis=0, keepdims=True)
            e = jnp.exp(s - top)
            pb = (e * (1.0 / jnp.sum(e, axis=0, keepdims=True))).astype(BF)
            pr[b * PAIRS + p] = pb
            o = dot(vals, pb, 0, 0)
            attnT[p * TILE : p * TILE + HDIM, b * TILE : (b + 1) * TILE] = o[
                0:HDIM, 0:TILE
            ].astype(BF)
            attnT[p * TILE + HDIM : (p + 1) * TILE, b * TILE : (b + 1) * TILE] = o[
                HDIM:, TILE:
            ].astype(BF)

    forward(1)
    halo_up.wait_recv()
    forward(0)
    halo_dn.wait_recv()
    forward(2)
    for e in range(EXT // TILE):
        kT[:, e * TILE : (e + 1) * TILE] = kv[e * TILE : (e + 1) * TILE, 0:D].T
    xnT[...] = xn[...].T
    load_wo.wait()

    def g_copy(b):
        return pltpu.make_async_remote_copy(
            gout.at[b], g_v.at[b], g_s.at[b], g_r.at[b],
            device_id=(before, dom), device_id_type=MESH,
        )

    rim_dn = pltpu.make_async_remote_copy(
        rim_lo, rim_next, rim_s.at[0], rim_r.at[0], device_id=(sec, prv), device_id_type=MESH
    )
    rim_up = pltpu.make_async_remote_copy(
        rim_hi, rim_prev, rim_s.at[1], rim_r.at[1], device_id=(sec, nxt), device_id_type=MESH
    )

    @pl.when(sec == SEC - 1)
    def _():
        load_g.wait()

    started = []

    def put(b, t, cols, val):
        rows = slice(t * TILE, (t + 1) * TILE)
        if t in started[-1][1]:
            acc[rows, cols] = acc[rows, cols] + val
        else:
            acc[rows, cols] = val

    done = set()
    for b in (0, 2, 1):
        @pl.when(sec < SEC - 1)
        def _():
            g_copy(b).wait_recv()

        da = dot(g_v[b], wo[...], 1, 1).astype(BF).astype(F32)
        for p in range(PAIRS):
            db = da[:, p * TILE : (p + 1) * TILE]
            da2[b * PAIRS + p, 0:TILE, :] = (db * m0).astype(BF)
            da2[b * PAIRS + p, TILE:, :] = (db * m1).astype(BF)
        started.append((b, set(done)))
        for p in range(PAIRS):
            vals = kv[b * TILE : b * TILE + KEYS, D + p * TILE : D + (p + 1) * TILE]
            d2 = da2[b * PAIRS + p]
            pb = pr[b * PAIRS + p]
            dp = dot(vals, d2, 1, 1)
            pf = pb.astype(F32)
            delta = jnp.sum(dp * pf, axis=0, keepdims=True)
            ds = (pf * (dp - delta)).astype(BF)
            dv = dot(pb, d2, 1, 0)
            dk = dot(ds, q2[b * PAIRS + p], 1, 0)
            for t in range(3):
                rows = slice(t * TILE, (t + 1) * TILE)
                put(b, b + t, slice(p * TILE, (p + 1) * TILE), dk[rows])
                put(b, b + t, slice(D + p * TILE, D + (p + 1) * TILE), dv[rows])
            dq = dot(kT[p * TILE : (p + 1) * TILE, b * TILE : b * TILE + KEYS], ds, 1, 0)
            dq = jnp.concatenate([dq[0:HDIM, 0:TILE], dq[HDIM:, TILE:]], axis=0)
            dqkv[b * TILE : (b + 1) * TILE, p * TILE : (p + 1) * TILE] = (dq.T * SCALE).astype(BF)
        done |= {b, b + 1, b + 2}
        if b == 0:
            rim_lo[...] = acc[0:TILE, :].astype(BF)
            rim_dn.start()
        if b == 2:
            rim_hi[...] = acc[EXT - TILE :, :].astype(BF)
            rim_up.start()

    for b in (0, 2, 1):
        rows = pl.ds(b * TILE, TILE)
        dkv = acc[(b + 1) * TILE : (b + 2) * TILE, :]
        if b == 0:
            rim_up.wait_recv()
            dkv = dkv + rim_prev[...].astype(F32)
        if b == 2:
            rim_dn.wait_recv()
            dkv = dkv + rim_next[...].astype(F32)
        dqkv[rows, D:] = dkv.astype(BF)
        dn = dot(dqkv[rows, :], wq[...], 1, 1)
        xh = xhat[rows, :]
        inv = inv_v[rows, 0:1]
        ln = inv * (
            dn
            - jnp.mean(dn, axis=-1, keepdims=True)
            - xh * jnp.mean(dn * xh, axis=-1, keepdims=True)
        )
        gout[b] = (g_v[b].astype(F32) + ln).astype(BF)

        @pl.when(sec > 0)
        def _():
            g_copy(b).start()

    store_g = pltpu.make_async_copy(gout, gout_hbm, out_sem)
    store_g.start()

    def c_copy(j):
        return pltpu.make_async_remote_copy(
            cs.at[j], cr.at[j], cs_s.at[j], cs_r.at[j],
            device_id=(sec, partner), device_id_type=MESH,
        )

    def y_copy(j, o):
        return pltpu.make_async_remote_copy(
            ys.at[j, o - 1], yr.at[j, o - 1], y_s.at[j, o - 1], y_r.at[j, o - 1],
            device_id=(sec, y_dev(o)), device_id_type=MESH,
        )

    def z_copy(j, o):
        return pltpu.make_async_remote_copy(
            zs.at[j, o - 1], zr.at[j, o - 1], z_s.at[j, o - 1], z_r.at[j, o - 1],
            device_id=(sec, z_dev(o)), device_id_type=MESH,
        )

    half = NY * NZ * 8
    order = (3, 0, 1, 2)
    for j in order:
        if j == 3:
            full = dot(attnT[...], g_v[...].reshape(ROWS, D), 1, 0)
        else:
            full = dot(xnT[...], dqkv[:, j * D : (j + 1) * D], 1, 0)
        gs[j] = full.reshape(NY * NZ, NC, 8, D)
        cs[j] = gs[j, :, 1 - c].reshape(half, D).astype(BF)
        c_copy(j).start()
    for j in order:
        c_copy(j).wait_recv()
        summed = gs[j, :, c] + cr[j].astype(F32).reshape(NY * NZ, 8, D)
        gs[j, :, 0] = summed
        for o in range(1, NY):
            to = lax.rem(y + o, NY)
            ys[j, o - 1] = gs[j, pl.ds(to * NZ, NZ), 0].reshape(NZ * 8, D).astype(BF)
            y_copy(j, o).start()
    for j in order:
        mine = gs[j, pl.ds(y * NZ, NZ), 0]
        for o in range(1, NY):
            y_copy(j, o).wait_recv()
            mine = mine + yr[j, o - 1].astype(F32).reshape(NZ, 8, D)
        gs[j, 0:NZ, 1] = mine
        for o in range(1, NZ):
            to = lax.rem(z + o, NZ)
            piece = gs[j, to, 1]
            zs[j, o - 1] = jnp.concatenate(
                [piece[:, 0 : D // 2], piece[:, D // 2 :]], axis=0
            ).astype(BF)
            z_copy(j, o).start()
    for j in order:
        own = gs[j, z, 1]
        total = jnp.concatenate([own[:, 0 : D // 2], own[:, D // 2 :]], axis=0)
        for o in range(1, NZ):
            z_copy(j, o).wait_recv()
            total = total + zr[j, o - 1].astype(F32)
        total = jnp.concatenate([total[0:8], total[8:16]], axis=1)
        if j == 3:
            dwo_ref[...] = total
        else:
            dwq_ref[:, j * D : (j + 1) * D] = total

    halo_up.wait_send()
    halo_dn.wait_send()
    rim_up.wait_send()
    rim_dn.wait_send()

    @pl.when(sec > 0)
    def _():
        for b in range(BLK):
            g_copy(b).wait_send()

    for j in range(COLS):
        c_copy(j).wait_send()
        for o in range(1, NY):
            y_copy(j, o).wait_send()
        for o in range(1, NZ):
            z_copy(j, o).wait_send()
    store_g.wait()


def local(layer_inputs, top_grad, w_qkv, w_out, neighbours):
    vm = pltpu.VMEM
    sem = pltpu.SemaphoreType.DMA
    anyspec = pl.BlockSpec(memory_space=pl.ANY)
    vspec = pl.BlockSpec(memory_space=pltpu.VMEM)
    gin, dwq, dwo = pl.pallas_call(
        body,
        out_shape=(
            jax.ShapeDtypeStruct((BLK, TILE, D), BF),
            jax.ShapeDtypeStruct((D // DOM, 3 * D), F32),
            jax.ShapeDtypeStruct((D // DOM, D), F32),
        ),
        in_specs=[pl.BlockSpec(memory_space=pltpu.SMEM)] + [anyspec] * 4,
        out_specs=(anyspec, vspec, vspec),
        scratch_shapes=[
            vm((ROWS, D), BF),
            vm((D, 3 * D), BF),
            vm((D, D), BF),
            vm((BLK, TILE, D), BF),
            vm((ROWS, D), F32),
            vm((ROWS, TILE), F32),
            vm((ROWS, D), BF),
            vm((D, ROWS), BF),
            vm((BLK * PAIRS, 2 * TILE, TILE), BF),
            vm((EXT, 2 * D), BF),
            vm((D, EXT), BF),
            vm((BLK * PAIRS, KEYS, 2 * TILE), BF),
            vm((D, ROWS), BF),
            vm((BLK * PAIRS, 2 * TILE, TILE), BF),
            vm((EXT, 2 * D), F32),
            vm((TILE, 2 * D), BF),
            vm((TILE, 2 * D), BF),
            vm((TILE, 2 * D), BF),
            vm((TILE, 2 * D), BF),
            vm((ROWS, 3 * D), BF),
            vm((BLK, TILE, D), BF),
            vm((COLS, NY * NZ, NC, 8, D), F32),
            vm((COLS, NY * NZ * 8, D), BF),
            vm((COLS, NY * NZ * 8, D), BF),
            vm((COLS, NY - 1, NZ * 8, D), BF),
            vm((COLS, NY - 1, NZ * 8, D), BF),
            vm((COLS, NZ - 1, 16, D // 2), BF),
            vm((COLS, NZ - 1, 16, D // 2), BF),
            sem((4,)), sem(()),
            sem((2,)), sem((2,)), sem((2,)), sem((2,)), sem((BLK,)), sem((BLK,)),
            sem((COLS,)), sem((COLS,)),
            sem((COLS, NY - 1)), sem((COLS, NY - 1)),
            sem((COLS, NZ - 1)), sem((COLS, NZ - 1)),
        ],
        compiler_params=pltpu.CompilerParams(
            collective_id=0, has_side_effects=True, vmem_limit_bytes=60 << 20
        ),
        name="layer_backward",
    )(
        neighbours,
        layer_inputs.reshape(ROWS, D),
        top_grad.reshape(BLK, TILE, D),
        w_qkv.reshape(D, 3 * D),
        w_out.reshape(D, D),
    )
    return (gin.reshape(1, 1, ROWS, D), dwq[None], dwo[None])


def solution(mesh):
    placed = (
        P("section", None, "dom", None),
        P(None, "dom", None),
        P("section", None, None),
        P("section", None, None),
        P("dom", None),
    )
    return jax.shard_map(
        local,
        mesh=mesh,
        in_specs=placed,
        out_specs=(
            P("section", None, "dom", None),
            P("section", "dom", None),
            P("section", "dom", None),
        ),
        check_vma=False,
    )
```

time: 757 us -> 97.9 us (0.13); the launches traced: 749 us -> 97.7 us
  matrix products: 279 us -> 0 us
  waiting for transfers between devices: 169 us -> 0 us
  local copies, waits for them, and re-layouts: 170 us -> 4.51 us
  Pallas kernels: 0 us -> 92.5 us
  other arithmetic: 84.4 us -> 0 us
  starting transfers between devices: 30.2 us -> 0 us
  between operations: 14.2 us -> 0.64 us
    dot_general x46 -> x0, matrix products: 279 us -> none  [the longest x4 102 us: layer_back(): jnp.einsum('bhqk,bqhd->bkhd', d_score, query, preferred_element_type=jnp....]
    reduce_scatter x1 -> x0, waiting for transfers between devices: 143 us -> none  [local(): lax.psum_scatter(jnp.concatenate([first_part, second_part], axis=-1), 'do...]
    pallas_call x0 -> x1, Pallas kernels: none -> 92.5 us  [local(): pl.pallas_call(body, out_shape=(jax.ShapeDtypeStruct((BLK, TILE, D), BF),...]
    scatter-add x12 -> x0, other arithmetic: 46.6 us -> none  [the longest x4 30.9 us: layer_back(): d_extended.at[where_at.reshape(-1)]]
    concatenate x12 -> x0, local copies, waits for them, and re-layouts: 41.8 us -> none  [the longest x8 34.1 us: layer_back(): jnp.concatenate([d_keys.reshape(blk, KMAX, tile, width), d_values.reshape...]
    transpose x8 -> x0, local copies, waits for them, and re-layouts: 33.7 us -> none  [the longest x4 20 us: layer_back(): jnp.einsum('bhqk,bqhd->bkhd', d_score, query, preferred_element_type=jnp....]
    slice x26 -> x0, local copies, waits for them, and re-layouts: 30.9 us -> none  [the longest x4 16.4 us: layer_back(): values = tiles[..., width:].reshape(blk, KMAX * tile, HEADS, hdim)]
    ppermute x14 -> x0, starting transfers between devices: 30.1 us -> none  [the longest x8 21 us: shifted(): return lax.ppermute(block, axis, route)]
  transfers between devices with their start and end apart: 15 -> 0, of which waited for: 7 -> 0; matrix products, arithmetic and copies ran while one was open for 21% -> 0% of each run, Pallas kernels for 0% -> 0%
where the time goes in v1:
time: 97.9 us; the launch traced here: 97.7 us
  Pallas kernels  92.5 us (94%)
  local copies, waits for them, and re-layouts  4.51 us (5%)
    pallas_call x1, Pallas kernels, local(): pl.pallas_call(body, out_shape=(jax.ShapeDtypeStruct((BLK, TILE, D), BF),...  92.5 us
    unnamed x3, local copies, waits for them, and re-layouts  4.51 us

profile of v1, /device:TPU:1, one launch (start us, length us, event | category | flops | bytes accessed | tf_op | source)
XLA Modules:
  0.0 97.7 jit_solution(10263255468791105681)
XLA Ops:
  0.6 92.5 %layer_backward.1 = (bf16[3,128,512]{2,1,0:T(8,128)(2,1)}, f32[8,1536]{1,0:T(8,128)}, f32[8,512]{1,0:T(8,128)}) custom-call(s32[3,3]{1,0:T(4,128)} %nbr.1, bf16[384,512]{1,0:T(8,128)(2,1)} %bitcast.9, bf16[3,128,512]{2,1,0:T(8,128)(2,1)} %bitcast.10, bf16[512,1536]{1,0:T(8,128)(2,1)} %bitcast.7, bf16[512,512]{1,0:T(8,128)(2,1)} %bitcast.8), custom_call_target="tpu_custom_call" | custom-call | tf_op jit(solution)/shard_map/layer_backward/pallas_call | solution.py:330
  93.1 1.8 %copy.11 = bf16[1,1,384,512]{3,2,1,0:T(8,128)(2,1)} copy(bf16[1,1,384,512]{3,2,1,0:T(8,128)(2,1)} %bitcast.11) | data formatting | bytes 786432
  94.9 1.4 %copy.12 = f32[1,8,1536]{2,1,0:T(8,128)} copy(f32[1,8,1536]{2,1,0:T(8,128)} %bitcast.12) | data formatting | bytes 98304
  96.3 1.3 %copy.13 = f32[1,8,512]{2,1,0:T(8,128)} copy(f32[1,8,512]{2,1,0:T(8,128)} %bitcast.13) | data formatting | bytes 32768

commit v2 on v1

v2 whole, which is shorter than its diff:
```python
import jax
import jax.numpy as jnp
from jax import lax
from jax.experimental import pallas as pl
from jax.experimental.pallas import tpu as pltpu
from jax.sharding import PartitionSpec as P

SEC = 4
NY, NZ, NC = 4, 8, 2
DOM = NY * NZ * NC
D = 512
HEADS = 8
HDIM = D // HEADS
PAIRS = HEADS // 2
TILE = 128
BLK = 3
KEYS = 3 * TILE
ROWS = BLK * TILE
EXT = ROWS + 2 * TILE
HALF = NY * NZ * 8
SCALE = 1.0 / HDIM**0.5
BF = jnp.bfloat16
F32 = jnp.float32
MESH = pl.DeviceIdType.MESH
CHUNKS = ((1536, 512, "z"), (0, 512, "y"), (512, 512, "y"), (1024, 256, "y"), (1280, 256, "z"))


def dot(a, b, ca, cb):
    return lax.dot_general(a, b, (((ca,), (cb,)), ((), ())), preferred_element_type=F32)


def body(
    nbr, x_hbm, g_hbm, wq_hbm, wo_hbm, gout_hbm, dwq_ref, dwo_ref,
    x_v, wq, wo, g_v, xhat, inv_v, xn, xnT, q2, kv, kvT, pr, attnT, da2, acc,
    rim_lo, rim_hi, rim_l, rim_r, dqkv, gout,
    in_sem, out_sem, halo_s, halo_r, rim_ss, rim_rs, g_s, g_r, cores, firsts, seconds,
):
    sec = lax.axis_index("section")
    dom = lax.axis_index("dom")
    y = lax.div(dom, NZ * NC)
    z = lax.rem(lax.div(dom, NC), NZ)
    c = lax.rem(dom, NC)
    left = lax.rem(dom + DOM - 1 + 2 * c, DOM)
    partner = dom + 1 - 2 * c
    before = lax.rem(sec + SEC - 1, SEC)
    after = lax.rem(sec + 1, SEC)

    def place(i):
        return i + c * (2 - 2 * i)

    def y_dev(o):
        return lax.rem(y + o, NY) * (NZ * NC) + z * NC + c

    def z_dev(o):
        return y * (NZ * NC) + lax.rem(z + o, NZ) * NC + c

    load_x = [pltpu.make_async_copy(x_hbm.at[place(i)], x_v.at[i], in_sem.at[i]) for i in range(BLK)]
    load_g = [
        pltpu.make_async_copy(g_hbm.at[place(i)], g_v.at[i], in_sem.at[BLK + i]) for i in range(BLK)
    ]
    load_wq = pltpu.make_async_copy(wq_hbm, wq, in_sem.at[2 * BLK])
    load_wo = pltpu.make_async_copy(wo_hbm, wo, in_sem.at[2 * BLK + 1])
    for copy in load_x:
        copy.start()
    load_wq.start()
    load_wo.start()

    @pl.when(sec == SEC - 1)
    def _():
        for copy in load_g:
            copy.start()

    barrier = pltpu.get_barrier_semaphore()
    peers = [(sec, left), (sec, partner), (before, dom), (after, dom)]
    peers += [(sec, y_dev(o)) for o in range(1, NY)]
    peers += [(sec, z_dev(o)) for o in range(1, NZ)]
    for peer in peers:
        pl.semaphore_signal(barrier, inc=1, device_id=peer, device_id_type=MESH)

    lane = lax.broadcasted_iota(jnp.int32, (1, TILE), 1)
    m0 = jnp.where(lane < HDIM, 1.0, 0.0)
    m1 = 1.0 - m0

    for b in range(BLK):
        load_x[b].wait()
        rows = pl.ds(b * TILE, TILE)
        xf = x_v[b].astype(F32)
        cen = xf - jnp.mean(xf, axis=-1, keepdims=True)
        inv = lax.rsqrt(jnp.mean(cen * cen, axis=-1, keepdims=True) + 1e-05)
        xh = cen * inv
        xhat[rows, :] = xh
        inv_v[rows, :] = jnp.broadcast_to(inv, (TILE, TILE))
        xn[rows, :] = xh.astype(BF)

    load_wq.wait()
    for h in range(2):
        part = dot(xn[...], wq[:, (1 + h) * D : (2 + h) * D], 1, 0)
        kv[TILE : TILE + ROWS, h * D : (h + 1) * D] = part.astype(BF)
    pl.semaphore_wait(barrier, len(peers))
    halo_l = pltpu.make_async_remote_copy(
        kv.at[pl.ds(TILE, TILE)], kv.at[pl.ds(0, TILE)], halo_s.at[0], halo_r.at[0],
        device_id=(sec, left), device_id_type=MESH,
    )
    halo_h = pltpu.make_async_remote_copy(
        kv.at[pl.ds(ROWS, TILE)], kv.at[pl.ds(TILE + ROWS, TILE)], halo_s.at[1], halo_r.at[1],
        device_id=(sec, partner), device_id_type=MESH,
    )
    halo_l.start()
    halo_h.start()

    qs = dot(xn[...], wq[:, 0:D], 1, 0).astype(BF).astype(F32) * SCALE
    for b in range(BLK):
        for p in range(PAIRS):
            qb = qs[b * TILE : (b + 1) * TILE, p * TILE : (p + 1) * TILE]
            q2[b * PAIRS + p, 0:TILE, :] = (qb * m0).astype(BF)
            q2[b * PAIRS + p, TILE:, :] = (qb * m1).astype(BF)

    def forward(b):
        spot = place(b)
        here = dom * BLK + spot
        low = lax.rem(here + DOM * BLK - 1 + 2 * c, DOM * BLK)
        high = lax.rem(here + DOM * BLK + 1 - 2 * c, DOM * BLK)
        n1 = jnp.full((TILE, 2 * TILE), nbr[spot, 1], jnp.int32)
        n2 = jnp.full((TILE, 2 * TILE), nbr[spot, 2], jnp.int32)
        has_low = (n1 == low) | (n2 == low)
        has_high = (n1 == high) | (n2 == high)
        for p in range(PAIRS):
            keys = kv[b * TILE : b * TILE + KEYS, p * TILE : (p + 1) * TILE]
            s = dot(keys, q2[b * PAIRS + p], 1, 1)
            s = jnp.concatenate(
                [
                    jnp.where(has_low, s[0:TILE], -1e30),
                    s[TILE : 2 * TILE],
                    jnp.where(has_high, s[2 * TILE :], -1e30),
                ],
                axis=0,
            )
            top = jnp.max(s, axis=0, keepdims=True)
            e = jnp.exp(s - top)
            pr[b * PAIRS + p] = (e * (1.0 / jnp.sum(e, axis=0, keepdims=True))).astype(BF)

    def flip(e, h):
        kvT[h * D : (h + 1) * D, e * TILE : (e + 1) * TILE] = kv[
            e * TILE : (e + 1) * TILE, h * D : (h + 1) * D
        ].T

    forward(1)
    for e in range(1, 4):
        flip(e, 0)
    halo_h.wait_recv()
    flip(4, 0)
    forward(2)
    halo_l.wait_recv()
    flip(0, 0)
    forward(0)
    load_wo.wait()

    def prepare():
        for e in range(EXT // TILE):
            flip(e, 1)
        for b in range(BLK):
            cols = slice(b * TILE, (b + 1) * TILE)
            for p in range(PAIRS):
                o = dot(
                    kvT[D + p * TILE : D + (p + 1) * TILE, b * TILE : b * TILE + KEYS],
                    pr[b * PAIRS + p], 1, 0,
                )
                o = jnp.concatenate([o[0:HDIM, 0:TILE], o[HDIM:, TILE:]], axis=0)
                o = o.reshape(TILE // 16, 2, 8, TILE)
                for s in range(2):
                    attnT[s, p * HDIM : (p + 1) * HDIM, cols] = (
                        o[:, s].reshape(HDIM, TILE).astype(BF)
                    )
            t = xhat[b * TILE : (b + 1) * TILE, :].T.reshape(HALF // 8, 2, 8, TILE)
            for s in range(2):
                xnT[s, :, cols] = t[:, s].reshape(HALF, TILE).astype(BF)

    @pl.when(sec < SEC - 1)
    def _():
        prepare()

    def g_copy(b):
        return pltpu.make_async_remote_copy(
            gout.at[b], g_v.at[b], g_s.at[b], g_r.at[b],
            device_id=(before, dom), device_id_type=MESH,
        )

    send_l = pltpu.make_async_remote_copy(
        rim_lo, rim_l, rim_ss.at[0], rim_rs.at[0], device_id=(sec, left), device_id_type=MESH
    )
    send_h = pltpu.make_async_remote_copy(
        rim_hi, rim_r, rim_ss.at[1], rim_rs.at[1], device_id=(sec, partner), device_id_type=MESH
    )

    def step(b):
        @pl.when(sec == SEC - 1)
        def _():
            load_g[b].wait()

        @pl.when(sec < SEC - 1)
        def _():
            g_copy(b).wait_recv()

        da = dot(g_v[b], wo[...], 1, 1).astype(BF).astype(F32)
        for p in range(PAIRS):
            db = da[:, p * TILE : (p + 1) * TILE]
            da2[b * PAIRS + p, 0:TILE, :] = (db * m0).astype(BF)
            da2[b * PAIRS + p, TILE:, :] = (db * m1).astype(BF)
        for p in range(PAIRS):
            vals = kv[b * TILE : b * TILE + KEYS, D + p * TILE : D + (p + 1) * TILE]
            d2 = da2[b * PAIRS + p]
            pb = pr[b * PAIRS + p]
            dp = dot(vals, d2, 1, 1)
            pf = pb.astype(F32)
            delta = jnp.sum(dp * pf, axis=0, keepdims=True)
            ds = (pf * (dp - delta)).astype(BF)
            for term, off in ((dot(pb, d2, 1, 0), D), (dot(ds, q2[b * PAIRS + p], 1, 0), 0)):
                cols = slice(off + p * TILE, off + (p + 1) * TILE)
                for t in range(3):
                    rows = slice((b + t) * TILE, (b + t + 1) * TILE)
                    val = term[t * TILE : (t + 1) * TILE]
                    if b == 0 or t == 2:
                        acc[rows, cols] = val
                    else:
                        acc[rows, cols] = acc[rows, cols] + val
            dq = dot(kvT[p * TILE : (p + 1) * TILE, b * TILE : b * TILE + KEYS], ds, 1, 0)
            dq = jnp.concatenate([dq[0:HDIM, 0:TILE], dq[HDIM:, TILE:]], axis=0)
            dqkv[b * TILE : (b + 1) * TILE, p * TILE : (p + 1) * TILE] = (dq.T * SCALE).astype(BF)

    def close(b):
        dkv = acc[(b + 1) * TILE : (b + 2) * TILE, :]
        if b == 0:
            send_l.wait_recv()
            dkv = dkv + rim_l[...].astype(F32)
        if b == 2:
            send_h.wait_recv()
            dkv = dkv + rim_r[...].astype(F32)
        dqkv[b * TILE : (b + 1) * TILE, D:] = dkv.astype(BF)

    def finish(b):
        rows = pl.ds(b * TILE, TILE)
        dn = dot(dqkv[rows, :], wq[...], 1, 1)
        xh = xhat[rows, :]
        inv = inv_v[rows, 0:1]
        ln = inv * (
            dn
            - jnp.mean(dn, axis=-1, keepdims=True)
            - xh * jnp.mean(dn * xh, axis=-1, keepdims=True)
        )
        gout[b] = (g_v[b].astype(F32) + ln).astype(BF)

    def store(b):
        return pltpu.make_async_copy(gout.at[b], gout_hbm.at[place(b)], out_sem.at[b])

    def pass_on(b):
        close(b)
        finish(b)
        g_copy(b).start()
        store(b).start()

    def c_copy(j):
        send, recv, _, ss, rs = cores[j]
        return pltpu.make_async_remote_copy(
            send, recv, ss, rs, device_id=(sec, partner), device_id_type=MESH
        )

    def axis_copy(j, stage, o):
        first = CHUNKS[j][2]
        axis = first if stage == 0 else ("z" if first == "y" else "y")
        send, recv, _, ss, rs = (firsts if stage == 0 else seconds)[j]
        to = y_dev(o) if axis == "y" else z_dev(o)
        return pltpu.make_async_remote_copy(
            send.at[o - 1], recv.at[o - 1], ss.at[o - 1], rs.at[o - 1],
            device_id=(sec, to), device_id_type=MESH,
        )

    def multiply(j, who):
        off, width, _ = CHUNKS[j]
        if off == 3 * D:
            return dot(attnT[who], g_v[...].reshape(ROWS, D), 1, 0)
        return dot(xnT[who], dqkv[:, off : off + width], 1, 0)

    def open_sum(j):
        cores[j][0][...] = multiply(j, 1 - c).astype(BF)
        c_copy(j).start()
        cores[j][2][...] = multiply(j, c).reshape(NY, NZ, 8, CHUNKS[j][1])

    def first_sum(j):
        width = CHUNKS[j][1]
        c_copy(j).wait_recv()
        held = cores[j][2]
        held[...] = held[...] + cores[j][1][...].astype(F32).reshape(NY, NZ, 8, width)
        send = firsts[j][0]
        if CHUNKS[j][2] == "y":
            for o in range(1, NY):
                send[o - 1] = held[lax.rem(y + o, NY)].reshape(NZ * 8, width).astype(BF)
                axis_copy(j, 0, o).start()
        else:
            for o in range(1, NZ):
                send[o - 1] = held[:, lax.rem(z + o, NZ)].reshape(NY * 8, width).astype(BF)
                axis_copy(j, 0, o).start()

    def fold(piece):
        width = piece.shape[1] // 2
        return jnp.concatenate([piece[:, 0:width], piece[:, width:]], axis=0)

    def second_sum(j):
        width = CHUNKS[j][1]
        held = cores[j][2]
        if CHUNKS[j][2] == "y":
            mine, n1, n2, me = held[y], NY, NZ, z
        else:
            mine, n1, n2, me = held[:, z], NZ, NY, y
        for o in range(1, n1):
            axis_copy(j, 0, o).wait_recv()
            mine = mine + firsts[j][1][o - 1].astype(F32).reshape(n2, 8, width)
        part = firsts[j][2]
        part[...] = mine
        for o in range(1, n2):
            seconds[j][0][o - 1] = fold(part[lax.rem(me + o, n2)]).astype(BF)
            axis_copy(j, 1, o).start()

    def end_sum(j):
        off, width, first = CHUNKS[j]
        me, n2 = (z, NZ) if first == "y" else (y, NY)
        total = fold(firsts[j][2][me])
        for o in range(1, n2):
            axis_copy(j, 1, o).wait_recv()
            total = total + seconds[j][1][o - 1].astype(F32)
        total = jnp.concatenate([total[0:8], total[8:16]], axis=1)
        if off == 3 * D:
            dwo_ref[...] = total
        else:
            dwq_ref[:, off : off + width] = total

    step(0)
    rim_lo[...] = acc[0:TILE, :].astype(BF)
    send_l.start()
    step(1)

    @pl.when(sec > 0)
    def _():
        pass_on(0)

    step(2)
    rim_hi[...] = acc[EXT - TILE :, :].astype(BF)
    send_h.start()

    @pl.when(sec > 0)
    def _():
        pass_on(1)
        pass_on(2)

        @pl.when(sec == SEC - 1)
        def _():
            prepare()

        for j in range(len(CHUNKS)):
            open_sum(j)
        for j in range(len(CHUNKS)):
            first_sum(j)

    @pl.when(sec == 0)
    def _():
        open_sum(0)
        open_sum(1)
        close(0)
        close(1)
        first_sum(0)
        first_sum(1)
        close(2)
        for j in range(2, len(CHUNKS)):
            open_sum(j)
        for j in range(2, len(CHUNKS)):
            first_sum(j)
        for b in range(BLK):
            finish(b)
            store(b).start()

    for j in range(len(CHUNKS)):
        second_sum(j)
    for j in range(len(CHUNKS)):
        end_sum(j)

    halo_l.wait_send()
    halo_h.wait_send()
    send_l.wait_send()
    send_h.wait_send()

    @pl.when(sec > 0)
    def _():
        for b in range(BLK):
            g_copy(b).wait_send()

    for j in range(len(CHUNKS)):
        c_copy(j).wait_send()
        for o in range(1, NY if CHUNKS[j][2] == "y" else NZ):
            axis_copy(j, 0, o).wait_send()
        for o in range(1, NZ if CHUNKS[j][2] == "y" else NY):
            axis_copy(j, 1, o).wait_send()
    for b in range(BLK):
        store(b).wait()


def copy_body(a, b, c, a_out, b_out, c_out, sem):
    copies = [
        pltpu.make_async_copy(src, dst, sem.at[i])
        for i, (src, dst) in enumerate(((a, a_out), (b, b_out), (c, c_out)))
    ]
    for copy in copies:
        copy.start()
    for copy in copies:
        copy.wait()


def local(layer_inputs, top_grad, w_qkv, w_out, neighbours):
    vm = pltpu.VMEM
    sem = pltpu.SemaphoreType.DMA
    anyspec = pl.BlockSpec(memory_space=pl.ANY)
    vspec = pl.BlockSpec(memory_space=pltpu.VMEM)
    outs = (
        jax.ShapeDtypeStruct((BLK, TILE, D), BF),
        jax.ShapeDtypeStruct((D // DOM, 3 * D), F32),
        jax.ShapeDtypeStruct((D // DOM, D), F32),
    )
    cores, firsts, seconds = [], [], []
    for _, width, first in CHUNKS:
        n1, n2 = (NY, NZ) if first == "y" else (NZ, NY)
        cores.append(
            (vm((HALF, width), BF), vm((HALF, width), BF), vm((NY, NZ, 8, width), F32), sem(()), sem(()))
        )
        firsts.append(
            (
                vm((n1 - 1, n2 * 8, width), BF), vm((n1 - 1, n2 * 8, width), BF),
                vm((n2, 8, width), F32), sem((n1 - 1,)), sem((n1 - 1,)),
            )
        )
        seconds.append(
            (
                vm((n2 - 1, 16, width // 2), BF), vm((n2 - 1, 16, width // 2), BF),
                vm((8, 128), F32), sem((n2 - 1,)), sem((n2 - 1,)),
            )
        )
    results = pl.pallas_call(
        body,
        out_shape=outs,
        in_specs=[pl.BlockSpec(memory_space=pltpu.SMEM)] + [anyspec] * 4,
        out_specs=(anyspec, vspec, vspec),
        scratch_shapes=[
            vm((BLK, TILE, D), BF),
            vm((D, 3 * D), BF),
            vm((D, D), BF),
            vm((BLK, TILE, D), BF),
            vm((ROWS, D), F32),
            vm((ROWS, TILE), F32),
            vm((ROWS, D), BF),
            vm((NC, HALF, ROWS), BF),
            vm((BLK * PAIRS, 2 * TILE, TILE), BF),
            vm((EXT, 2 * D), BF),
            vm((2 * D, EXT), BF),
            vm((BLK * PAIRS, KEYS, 2 * TILE), BF),
            vm((NC, HALF, ROWS), BF),
            vm((BLK * PAIRS, 2 * TILE, TILE), BF),
            vm((EXT, 2 * D), F32),
            vm((TILE, 2 * D), BF),
            vm((TILE, 2 * D), BF),
            vm((TILE, 2 * D), BF),
            vm((TILE, 2 * D), BF),
            vm((ROWS, 3 * D), BF),
            vm((BLK, TILE, D), BF),
            sem((2 * BLK + 2,)), sem((BLK,)),
            sem((2,)), sem((2,)), sem((2,)), sem((2,)), sem((BLK,)), sem((BLK,)),
            cores, firsts, seconds,
        ],
        compiler_params=pltpu.CompilerParams(
            collective_id=0, has_side_effects=True, vmem_limit_bytes=60 << 20
        ),
        name="layer_backward",
    )(
        neighbours,
        layer_inputs.reshape(BLK, TILE, D),
        top_grad.reshape(BLK, TILE, D),
        w_qkv.reshape(D, 3 * D),
        w_out.reshape(D, D),
    )
    gin, dwq, dwo = pl.pallas_call(
        copy_body,
        out_shape=outs,
        in_specs=[anyspec] * 3,
        out_specs=(anyspec,) * 3,
        scratch_shapes=[sem((3,))],
        name="results",
    )(*results)
    return (gin.reshape(1, 1, ROWS, D), dwq[None], dwo[None])


def solution(mesh):
    placed = (
        P("section", None, "dom", None),
        P(None, "dom", None),
        P("section", None, None),
        P("section", None, None),
        P("dom", None),
    )
    return jax.shard_map(
        local,
        mesh=mesh,
        in_specs=placed,
        out_specs=(
            P("section", None, "dom", None),
            P("section", "dom", None),
            P("section", "dom", None),
        ),
        check_vma=False,
    )
```

time: 97.9 us -> 100 us (1.021)
  Pallas kernels: 92.5 us -> 99.3 us
  local copies, waits for them, and re-layouts: 4.51 us -> 0 us
    pallas_call x1 -> x2, Pallas kernels: 92.5 us -> 99.3 us  [the longest x1 84.2 us: local(): pl.pallas_call(body, out_shape=outs, in_specs=[pl.BlockSpec(memory_space=...]
    unnamed x3 -> x0, local copies, waits for them, and re-layouts: 4.51 us -> none
where the time goes in v2:
time: 100 us
  Pallas kernels  99.3 us (99%)
    pallas_call x1, Pallas kernels, local(): pl.pallas_call(body, out_shape=outs, in_specs=[pl.BlockSpec(memory_space=...  84.2 us
    pallas_call x1, Pallas kernels, local(): pl.pallas_call(copy_body, out_shape=outs, in_specs=[anyspec] * 3, out_spe...  15 us

profile of v2, /device:TPU:1, one launch (start us, length us, event | category | flops | bytes accessed | tf_op | source)
XLA Modules:
  0.0 100.1 jit_solution(10494076718390794419)
XLA Ops:
  0.6 84.2 %layer_backward.1 = (bf16[3,128,512]{2,1,0:T(8,128)(2,1)}, f32[8,1536]{1,0:T(8,128)}, f32[8,512]{1,0:T(8,128)}) custom-call(s32[3,3]{1,0:T(4,128)} %nbr.1, bf16[3,128,512]{2,1,0:T(8,128)(2,1)} %bitcast.9, bf16[3,128,512]{2,1,0:T(8,128)(2,1)} %bitcast.10, bf16[512,1536]{1,0:T(8,128)(2,1)} %bitcast.7, bf16[512,512]{1,0:T(8,128)(2,1)} %bitcast.8), custom_call_target="tpu_custom_call" | custom-call | tf_op jit(solution)/shard_map/layer_backward/pallas_call | solution.py:444
  84.9 15.0 %results.1 = (bf16[3,128,512]{2,1,0:T(8,128)(2,1)}, f32[8,1536]{1,0:T(8,128)}, f32[8,512]{1,0:T(8,128)}) custom-call(bf16[3,128,512]{2,1,0:T(8,128)(2,1)} %get-tuple-element.9.a, f32[8,1536]{1,0:T(8,128)} %get-tuple-element.10.b, f32[8,512]{1,0:T(8,128)} %get-tuple-element.11.c), custom_call_target="tpu_custom_call" | custom-call | tf_op jit(solution)/shard_map/results/pallas_call | solution.py:486

commit v3 on v2

--- a/solution.py
+++ b/solution.py
@@ -22,7 +22,7 @@
 BF = jnp.bfloat16
 F32 = jnp.float32
 MESH = pl.DeviceIdType.MESH
-CHUNKS = ((1536, 512, "z"), (0, 512, "y"), (512, 512, "y"), (1024, 256, "y"), (1280, 256, "z"))
+CHUNKS = ((1536, 512, "y"), (0, 512, "y"), (512, 512, "y"), (1024, 256, "y"), (1280, 256, "z"))
 
 
 def dot(a, b, ca, cb):
@@ -32,7 +32,7 @@
 def body(
     nbr, x_hbm, g_hbm, wq_hbm, wo_hbm, gout_hbm, dwq_ref, dwo_ref,
     x_v, wq, wo, g_v, xhat, inv_v, xn, xnT, q2, kv, kvT, pr, attnT, da2, acc,
-    rim_lo, rim_hi, rim_l, rim_r, dqkv, gout,
+    rim_out, rim_in, accb, dqkv, gout,
     in_sem, out_sem, halo_s, halo_r, rim_ss, rim_rs, g_s, g_r, cores, firsts, seconds,
 ):
     sec = lax.axis_index("section")
@@ -40,13 +40,13 @@
     y = lax.div(dom, NZ * NC)
     z = lax.rem(lax.div(dom, NC), NZ)
     c = lax.rem(dom, NC)
-    left = lax.rem(dom + DOM - 1 + 2 * c, DOM)
+    other = lax.rem(dom + DOM - 1 + 2 * c, DOM)
     partner = dom + 1 - 2 * c
     before = lax.rem(sec + SEC - 1, SEC)
     after = lax.rem(sec + 1, SEC)
 
     def place(i):
-        return i + c * (2 - 2 * i)
+        return i + (1 - c) * (2 - 2 * i)
 
     def y_dev(o):
         return lax.rem(y + o, NY) * (NZ * NC) + z * NC + c
@@ -71,7 +71,7 @@
             copy.start()
 
     barrier = pltpu.get_barrier_semaphore()
-    peers = [(sec, left), (sec, partner), (before, dom), (after, dom)]
+    peers = [(sec, other), (sec, partner), (before, dom), (after, dom)]
     peers += [(sec, y_dev(o)) for o in range(1, NY)]
     peers += [(sec, z_dev(o)) for o in range(1, NZ)]
     for peer in peers:
@@ -84,31 +84,36 @@
     for b in range(BLK):
         load_x[b].wait()
         rows = pl.ds(b * TILE, TILE)
+        own = pl.ds((b + 1) * TILE, TILE)
         xf = x_v[b].astype(F32)
         cen = xf - jnp.mean(xf, axis=-1, keepdims=True)
         inv = lax.rsqrt(jnp.mean(cen * cen, axis=-1, keepdims=True) + 1e-05)
         xh = cen * inv
         xhat[rows, :] = xh
         inv_v[rows, :] = jnp.broadcast_to(inv, (TILE, TILE))
-        xn[rows, :] = xh.astype(BF)
+        xn[own, :] = xh.astype(BF)
 
     load_wq.wait()
     for h in range(2):
-        part = dot(xn[...], wq[:, (1 + h) * D : (2 + h) * D], 1, 0)
+        part = dot(xn[TILE : TILE + ROWS, :], wq[:, (1 + h) * D : (2 + h) * D], 1, 0)
         kv[TILE : TILE + ROWS, h * D : (h + 1) * D] = part.astype(BF)
     pl.semaphore_wait(barrier, len(peers))
-    halo_l = pltpu.make_async_remote_copy(
-        kv.at[pl.ds(TILE, TILE)], kv.at[pl.ds(0, TILE)], halo_s.at[0], halo_r.at[0],
-        device_id=(sec, left), device_id_type=MESH,
-    )
-    halo_h = pltpu.make_async_remote_copy(
-        kv.at[pl.ds(ROWS, TILE)], kv.at[pl.ds(TILE + ROWS, TILE)], halo_s.at[1], halo_r.at[1],
-        device_id=(sec, partner), device_id_type=MESH,
-    )
-    halo_l.start()
-    halo_h.start()
-
-    qs = dot(xn[...], wq[:, 0:D], 1, 0).astype(BF).astype(F32) * SCALE
+    def halo(ref, side):
+        sem, to = (0, partner) if side == 0 else (1, other)
+        source, target = (TILE, 0) if side == 0 else (ROWS, TILE + ROWS)
+        if ref is xn:
+            sem = sem + 2
+        return pltpu.make_async_remote_copy(
+            ref.at[pl.ds(source, TILE)], ref.at[pl.ds(target, TILE)],
+            halo_s.at[sem], halo_r.at[sem], device_id=(sec, to), device_id_type=MESH,
+        )
+
+    halo(kv, 1).start()
+    halo(kv, 0).start()
+    halo(xn, 0).start()
+    halo(xn, 1).start()
+
+    qs = dot(xn[TILE : TILE + ROWS, :], wq[:, 0:D], 1, 0).astype(BF).astype(F32) * SCALE
     for b in range(BLK):
         for p in range(PAIRS):
             qb = qs[b * TILE : (b + 1) * TILE, p * TILE : (p + 1) * TILE]
@@ -118,8 +123,8 @@
     def forward(b):
         spot = place(b)
         here = dom * BLK + spot
-        low = lax.rem(here + DOM * BLK - 1 + 2 * c, DOM * BLK)
-        high = lax.rem(here + DOM * BLK + 1 - 2 * c, DOM * BLK)
+        low = lax.rem(here + DOM * BLK + 1 - 2 * c, DOM * BLK)
+        high = lax.rem(here + DOM * BLK - 1 + 2 * c, DOM * BLK)
         n1 = jnp.full((TILE, 2 * TILE), nbr[spot, 1], jnp.int32)
         n2 = jnp.full((TILE, 2 * TILE), nbr[spot, 2], jnp.int32)
         has_low = (n1 == low) | (n2 == low)
@@ -144,20 +149,28 @@
             e * TILE : (e + 1) * TILE, h * D : (h + 1) * D
         ].T
 
+    def forward_last():
+        halo(kv, 1).wait_recv()
+        flip(4, 0)
+        forward(2)
+
     forward(1)
     for e in range(1, 4):
         flip(e, 0)
-    halo_h.wait_recv()
-    flip(4, 0)
-    forward(2)
-    halo_l.wait_recv()
+    halo(kv, 0).wait_recv()
     flip(0, 0)
     forward(0)
     load_wo.wait()
 
     def prepare():
+        halo(xn, 0).wait_recv()
+        halo(xn, 1).wait_recv()
         for e in range(EXT // TILE):
             flip(e, 1)
+            cols = slice(e * TILE, (e + 1) * TILE)
+            t = xn[cols, :].astype(F32).T.reshape(HALF // 8, 2, 8, TILE)
+            for s in range(2):
+                xnT[s, :, cols] = t[:, s].reshape(HALF, TILE).astype(BF)
         for b in range(BLK):
             cols = slice(b * TILE, (b + 1) * TILE)
             for p in range(PAIRS):
@@ -171,12 +184,10 @@
                     attnT[s, p * HDIM : (p + 1) * HDIM, cols] = (
                         o[:, s].reshape(HDIM, TILE).astype(BF)
                     )
-            t = xhat[b * TILE : (b + 1) * TILE, :].T.reshape(HALF // 8, 2, 8, TILE)
-            for s in range(2):
-                xnT[s, :, cols] = t[:, s].reshape(HALF, TILE).astype(BF)
 
     @pl.when(sec < SEC - 1)
     def _():
+        forward_last()
         prepare()
 
     def g_copy(b):
@@ -185,12 +196,11 @@
             device_id=(before, dom), device_id_type=MESH,
         )
 
-    send_l = pltpu.make_async_remote_copy(
-        rim_lo, rim_l, rim_ss.at[0], rim_rs.at[0], device_id=(sec, left), device_id_type=MESH
-    )
-    send_h = pltpu.make_async_remote_copy(
-        rim_hi, rim_r, rim_ss.at[1], rim_rs.at[1], device_id=(sec, partner), device_id_type=MESH
-    )
+    def rim(side, h):
+        return pltpu.make_async_remote_copy(
+            rim_out.at[side, h], rim_in.at[side, h], rim_ss.at[side, h], rim_rs.at[side, h],
+            device_id=(sec, partner if side == 0 else other), device_id_type=MESH,
+        )
 
     def step(b):
         @pl.when(sec == SEC - 1)
@@ -226,15 +236,28 @@
             dq = dot(kvT[p * TILE : (p + 1) * TILE, b * TILE : b * TILE + KEYS], ds, 1, 0)
             dq = jnp.concatenate([dq[0:HDIM, 0:TILE], dq[HDIM:, TILE:]], axis=0)
             dqkv[b * TILE : (b + 1) * TILE, p * TILE : (p + 1) * TILE] = (dq.T * SCALE).astype(BF)
+            if b != 1 and p % 2 == 1:
+                side, h = b // 2, p // 2
+                rows = slice(side * (EXT - TILE), side * (EXT - TILE) + TILE)
+                for off in range(2):
+                    start = off * D + h * (D // 2)
+                    rim_out[side, h, :, off * (D // 2) : (off + 1) * (D // 2)] = acc[
+                        rows, start : start + D // 2
+                    ].astype(BF)
+                rim(side, h).start()
 
     def close(b):
         dkv = acc[(b + 1) * TILE : (b + 2) * TILE, :]
-        if b == 0:
-            send_l.wait_recv()
-            dkv = dkv + rim_l[...].astype(F32)
-        if b == 2:
-            send_h.wait_recv()
-            dkv = dkv + rim_r[...].astype(F32)
+        if b != 1:
+            side = b // 2
+            rim(side, 0).wait_recv()
+            rim(side, 1).wait_recv()
+            terms = [
+                rim_in[side, h, :, off * (D // 2) : (off + 1) * (D // 2)].astype(F32)
+                for off in range(2)
+                for h in range(2)
+            ]
+            dkv = dkv + jnp.concatenate(terms, axis=1)
         dqkv[b * TILE : (b + 1) * TILE, D:] = dkv.astype(BF)
 
     def finish(b):
@@ -267,7 +290,8 @@
     def axis_copy(j, stage, o):
         first = CHUNKS[j][2]
         axis = first if stage == 0 else ("z" if first == "y" else "y")
-        send, recv, _, ss, rs = (firsts if stage == 0 else seconds)[j]
+        refs = (firsts if stage == 0 else seconds)[j]
+        send, recv, ss, rs = refs[0], refs[1], refs[-2], refs[-1]
         to = y_dev(o) if axis == "y" else z_dev(o)
         return pltpu.make_async_remote_copy(
             send.at[o - 1], recv.at[o - 1], ss.at[o - 1], rs.at[o - 1],
@@ -278,7 +302,9 @@
         off, width, _ = CHUNKS[j]
         if off == 3 * D:
             return dot(attnT[who], g_v[...].reshape(ROWS, D), 1, 0)
-        return dot(xnT[who], dqkv[:, off : off + width], 1, 0)
+        if off == 0:
+            return dot(xnT[who, :, TILE : TILE + ROWS], dqkv[:, 0:D], 1, 0)
+        return dot(xnT[who], accb[:, off - D : off - D + width], 1, 0)
 
     def open_sum(j):
         cores[j][0][...] = multiply(j, 1 - c).astype(BF)
@@ -334,17 +360,17 @@
             dwq_ref[:, off : off + width] = total
 
     step(0)
-    rim_lo[...] = acc[0:TILE, :].astype(BF)
-    send_l.start()
     step(1)
 
     @pl.when(sec > 0)
     def _():
         pass_on(0)
 
+    @pl.when(sec == SEC - 1)
+    def _():
+        forward_last()
+
     step(2)
-    rim_hi[...] = acc[EXT - TILE :, :].astype(BF)
-    send_h.start()
 
     @pl.when(sec > 0)
     def _():
@@ -355,25 +381,18 @@
         def _():
             prepare()
 
-        for j in range(len(CHUNKS)):
-            open_sum(j)
-        for j in range(len(CHUNKS)):
-            first_sum(j)
+    for h in range(4):
+        cols = slice(h * (D // 2), (h + 1) * (D // 2))
+        accb[:, cols] = acc[:, cols].astype(BF)
+    for j in range(len(CHUNKS)):
+        open_sum(j)
+    for j in range(len(CHUNKS)):
+        first_sum(j)
 
     @pl.when(sec == 0)
     def _():
-        open_sum(0)
-        open_sum(1)
-        close(0)
-        close(1)
-        first_sum(0)
-        first_sum(1)
-        close(2)
-        for j in range(2, len(CHUNKS)):
-            open_sum(j)
-        for j in range(2, len(CHUNKS)):
-            first_sum(j)
         for b in range(BLK):
+            close(b)
             finish(b)
             store(b).start()
 
@@ -382,10 +401,11 @@
     for j in range(len(CHUNKS)):
         end_sum(j)
 
-    halo_l.wait_send()
-    halo_h.wait_send()
-    send_l.wait_send()
-    send_h.wait_send()
+    for side in range(2):
+        halo(kv, side).wait_send()
+        halo(xn, side).wait_send()
+        rim(side, 0).wait_send()
+        rim(side, 1).wait_send()
 
     @pl.when(sec > 0)
     def _():
@@ -402,15 +422,10 @@
         store(b).wait()
 
 
-def copy_body(a, b, c, a_out, b_out, c_out, sem):
-    copies = [
-        pltpu.make_async_copy(src, dst, sem.at[i])
-        for i, (src, dst) in enumerate(((a, a_out), (b, b_out), (c, c_out)))
-    ]
-    for copy in copies:
-        copy.start()
-    for copy in copies:
-        copy.wait()
+def copy_body(a, b, c, a_out, b_out, c_out):
+    a_out[...] = a[...]
+    b_out[...] = b[...]
+    c_out[...] = c[...]
 
 
 def local(layer_inputs, top_grad, w_qkv, w_out, neighbours):
@@ -438,7 +453,7 @@
         seconds.append(
             (
                 vm((n2 - 1, 16, width // 2), BF), vm((n2 - 1, 16, width // 2), BF),
-                vm((8, 128), F32), sem((n2 - 1,)), sem((n2 - 1,)),
+                sem((n2 - 1,)), sem((n2 - 1,)),
             )
         )
     results = pl.pallas_call(
@@ -453,8 +468,8 @@
             vm((BLK, TILE, D), BF),
             vm((ROWS, D), F32),
             vm((ROWS, TILE), F32),
-            vm((ROWS, D), BF),
-            vm((NC, HALF, ROWS), BF),
+            vm((EXT, D), BF),
+            vm((NC, HALF, EXT), BF),
             vm((BLK * PAIRS, 2 * TILE, TILE), BF),
             vm((EXT, 2 * D), BF),
             vm((2 * D, EXT), BF),
@@ -462,14 +477,13 @@
             vm((NC, HALF, ROWS), BF),
             vm((BLK * PAIRS, 2 * TILE, TILE), BF),
             vm((EXT, 2 * D), F32),
-            vm((TILE, 2 * D), BF),
-            vm((TILE, 2 * D), BF),
-            vm((TILE, 2 * D), BF),
-            vm((TILE, 2 * D), BF),
+            vm((2, 2, TILE, D), BF),
+            vm((2, 2, TILE, D), BF),
+            vm((EXT, 2 * D), BF),
             vm((ROWS, 3 * D), BF),
             vm((BLK, TILE, D), BF),
             sem((2 * BLK + 2,)), sem((BLK,)),
-            sem((2,)), sem((2,)), sem((2,)), sem((2,)), sem((BLK,)), sem((BLK,)),
+            sem((4,)), sem((4,)), sem((2, 2)), sem((2, 2)), sem((BLK,)), sem((BLK,)),
             cores, firsts, seconds,
         ],
         compiler_params=pltpu.CompilerParams(
@@ -486,9 +500,8 @@
     gin, dwq, dwo = pl.pallas_call(
         copy_body,
         out_shape=outs,
-        in_specs=[anyspec] * 3,
-        out_specs=(anyspec,) * 3,
-        scratch_shapes=[sem((3,))],
+        in_specs=[vspec] * 3,
+        out_specs=(vspec,) * 3,
         name="results",
     )(*results)
     return (gin.reshape(1, 1, ROWS, D), dwq[None], dwo[None])

time: 100 us -> 79.4 us (0.79)
  Pallas kernels: 99.3 us -> 78.6 us
    pallas_call x1, Pallas kernels: 15 us -> 1.81 us  [local(): pl.pallas_call(copy_body, out_shape=outs, in_specs=[vspec] * 3, out_specs...]
    pallas_call x1, Pallas kernels: 84.2 us -> 76.8 us  [local(): pl.pallas_call(body, out_shape=outs, in_specs=[pl.BlockSpec(memory_space=...]
where the time goes in v3:
time: 79.4 us; the launch traced here: 79.3 us
  Pallas kernels  78.6 us (99%)
    pallas_call x1, Pallas kernels, local(): pl.pallas_call(body, out_shape=outs, in_specs=[pl.BlockSpec(memory_space=...  76.8 us
    pallas_call x1, Pallas kernels, local(): pl.pallas_call(copy_body, out_shape=outs, in_specs=[vspec] * 3, out_specs...  1.81 us

profile of v3, /device:TPU:1, one launch (start us, length us, event | category | flops | bytes accessed | tf_op | source)
XLA Modules:
  0.0 79.3 jit_solution(12907124694180605216)
XLA Ops:
  0.6 76.8 %layer_backward.1 = (bf16[3,128,512]{2,1,0:T(8,128)(2,1)}, f32[8,1536]{1,0:T(8,128)}, f32[8,512]{1,0:T(8,128)}) custom-call(s32[3,3]{1,0:T(4,128)} %nbr.1, bf16[3,128,512]{2,1,0:T(8,128)(2,1)} %bitcast.9, bf16[3,128,512]{2,1,0:T(8,128)(2,1)} %bitcast.10, bf16[512,1536]{1,0:T(8,128)(2,1)} %bitcast.7, bf16[512,512]{1,0:T(8,128)(2,1)} %bitcast.8), custom_call_target="tpu_custom_call" | custom-call | tf_op jit(solution)/shard_map/layer_backward/pallas_call | solution.py:459
  77.5 1.8 %results.1 = (bf16[3,128,512]{2,1,0:T(8,128)(2,1)}, f32[8,1536]{1,0:T(8,128)}, f32[8,512]{1,0:T(8,128)}) custom-call(bf16[3,128,512]{2,1,0:T(8,128)(2,1)} %get-tuple-element.9.a, f32[8,1536]{1,0:T(8,128)} %get-tuple-element.10.b, f32[8,512]{1,0:T(8,128)} %get-tuple-element.11.c), custom_call_target="tpu_custom_call" | custom-call | tf_op jit(solution)/shard_map/results/pallas_call | solution.py:500

commit v4 on v3

--- a/solution.py
+++ b/solution.py
@@ -22,7 +22,7 @@
 BF = jnp.bfloat16
 F32 = jnp.float32
 MESH = pl.DeviceIdType.MESH
-CHUNKS = ((1536, 512, "y"), (0, 512, "y"), (512, 512, "y"), (1024, 256, "y"), (1280, 256, "z"))
+CHUNKS = ((1536, 512, "y"), (1024, 512, "z"), (0, 512, "y"), (512, 512, "y"))
 
 
 def dot(a, b, ca, cb):
@@ -32,7 +32,7 @@
 def body(
     nbr, x_hbm, g_hbm, wq_hbm, wo_hbm, gout_hbm, dwq_ref, dwo_ref,
     x_v, wq, wo, g_v, xhat, inv_v, xn, xnT, q2, kv, kvT, pr, attnT, da2, acc,
-    rim_out, rim_in, accb, dqkv, gout,
+    rim_out, rim_in, accb, dsc, dqkv, gout,
     in_sem, out_sem, halo_s, halo_r, rim_ss, rim_rs, g_s, g_r, cores, firsts, seconds,
 ):
     sec = lax.axis_index("section")
@@ -202,7 +202,7 @@
             device_id=(sec, partner if side == 0 else other), device_id_type=MESH,
         )
 
-    def step(b):
+    def wait_g(b):
         @pl.when(sec == SEC - 1)
         def _():
             load_g[b].wait()
@@ -211,40 +211,52 @@
         def _():
             g_copy(b).wait_recv()
 
+    def step(b):
         da = dot(g_v[b], wo[...], 1, 1).astype(BF).astype(F32)
         for p in range(PAIRS):
             db = da[:, p * TILE : (p + 1) * TILE]
             da2[b * PAIRS + p, 0:TILE, :] = (db * m0).astype(BF)
             da2[b * PAIRS + p, TILE:, :] = (db * m1).astype(BF)
+
+        def add(slots, term, off, p):
+            cols = slice(off + p * TILE, off + (p + 1) * TILE)
+            for n, t in enumerate(slots):
+                rows = slice((b + t) * TILE, (b + t + 1) * TILE)
+                val = term[n * TILE : (n + 1) * TILE]
+                if b == 0 or t == 2:
+                    acc[rows, cols] = val
+                else:
+                    acc[rows, cols] = acc[rows, cols] + val
+
+        edge, rest = {0: ((0,), (1, 2)), 1: ((), (0, 1, 2)), 2: ((2,), (0, 1))}[b]
+        at = slice(0, 0) if b == 1 else slice(edge[0] * TILE, (edge[0] + 1) * TILE)
+        inner = slice(rest[0] * TILE, (rest[-1] + 1) * TILE)
+        side = b // 2
+        if b != 1:
+            for p in range(PAIRS):
+                term = dot(pr[b * PAIRS + p, at, :], da2[b * PAIRS + p], 1, 0)
+                add(edge, term, D, p)
+                rim_out[side, 1, :, p * TILE : (p + 1) * TILE] = term.astype(BF)
+            rim(side, 1).start()
         for p in range(PAIRS):
             vals = kv[b * TILE : b * TILE + KEYS, D + p * TILE : D + (p + 1) * TILE]
-            d2 = da2[b * PAIRS + p]
-            pb = pr[b * PAIRS + p]
-            dp = dot(vals, d2, 1, 1)
-            pf = pb.astype(F32)
+            dp = dot(vals, da2[b * PAIRS + p], 1, 1)
+            pf = pr[b * PAIRS + p].astype(F32)
             delta = jnp.sum(dp * pf, axis=0, keepdims=True)
             ds = (pf * (dp - delta)).astype(BF)
-            for term, off in ((dot(pb, d2, 1, 0), D), (dot(ds, q2[b * PAIRS + p], 1, 0), 0)):
-                cols = slice(off + p * TILE, off + (p + 1) * TILE)
-                for t in range(3):
-                    rows = slice((b + t) * TILE, (b + t + 1) * TILE)
-                    val = term[t * TILE : (t + 1) * TILE]
-                    if b == 0 or t == 2:
-                        acc[rows, cols] = val
-                    else:
-                        acc[rows, cols] = acc[rows, cols] + val
-            dq = dot(kvT[p * TILE : (p + 1) * TILE, b * TILE : b * TILE + KEYS], ds, 1, 0)
+            dsc[p] = ds
+            if b != 1:
+                term = dot(ds[at], q2[b * PAIRS + p], 1, 0)
+                add(edge, term, 0, p)
+                rim_out[side, 0, :, p * TILE : (p + 1) * TILE] = term.astype(BF)
+        if b != 1:
+            rim(side, 0).start()
+        for p in range(PAIRS):
+            add(rest, dot(pr[b * PAIRS + p, inner, :], da2[b * PAIRS + p], 1, 0), D, p)
+            add(rest, dot(dsc[p, inner, :], q2[b * PAIRS + p], 1, 0), 0, p)
+            dq = dot(kvT[p * TILE : (p + 1) * TILE, b * TILE : b * TILE + KEYS], dsc[p], 1, 0)
             dq = jnp.concatenate([dq[0:HDIM, 0:TILE], dq[HDIM:, TILE:]], axis=0)
             dqkv[b * TILE : (b + 1) * TILE, p * TILE : (p + 1) * TILE] = (dq.T * SCALE).astype(BF)
-            if b != 1 and p % 2 == 1:
-                side, h = b // 2, p // 2
-                rows = slice(side * (EXT - TILE), side * (EXT - TILE) + TILE)
-                for off in range(2):
-                    start = off * D + h * (D // 2)
-                    rim_out[side, h, :, off * (D // 2) : (off + 1) * (D // 2)] = acc[
-                        rows, start : start + D // 2
-                    ].astype(BF)
-                rim(side, h).start()
 
     def close(b):
         dkv = acc[(b + 1) * TILE : (b + 2) * TILE, :]
@@ -252,12 +264,7 @@
             side = b // 2
             rim(side, 0).wait_recv()
             rim(side, 1).wait_recv()
-            terms = [
-                rim_in[side, h, :, off * (D // 2) : (off + 1) * (D // 2)].astype(F32)
-                for off in range(2)
-                for h in range(2)
-            ]
-            dkv = dkv + jnp.concatenate(terms, axis=1)
+            dkv = dkv + jnp.concatenate([rim_in[side, 0], rim_in[side, 1]], axis=1).astype(F32)
         dqkv[b * TILE : (b + 1) * TILE, D:] = dkv.astype(BF)
 
     def finish(b):
@@ -359,7 +366,9 @@
         else:
             dwq_ref[:, off : off + width] = total
 
+    wait_g(0)
     step(0)
+    wait_g(1)
     step(1)
 
     @pl.when(sec > 0)
@@ -369,6 +378,15 @@
     @pl.when(sec == SEC - 1)
     def _():
         forward_last()
+
+    @pl.when(sec == 0)
+    def _():
+        wait_g(2)
+        open_sum(0)
+
+    @pl.when(sec > 0)
+    def _():
+        wait_g(2)
 
     step(2)
 
@@ -381,10 +399,12 @@
         def _():
             prepare()
 
-    for h in range(4):
+        open_sum(0)
+
+    for h in (2, 3, 0, 1):
         cols = slice(h * (D // 2), (h + 1) * (D // 2))
         accb[:, cols] = acc[:, cols].astype(BF)
-    for j in range(len(CHUNKS)):
+    for j in range(1, len(CHUNKS)):
         open_sum(j)
     for j in range(len(CHUNKS)):
         first_sum(j)
@@ -480,6 +500,7 @@
             vm((2, 2, TILE, D), BF),
             vm((2, 2, TILE, D), BF),
             vm((EXT, 2 * D), BF),
+            vm((PAIRS, KEYS, 2 * TILE), BF),
             vm((ROWS, 3 * D), BF),
             vm((BLK, TILE, D), BF),
             sem((2 * BLK + 2,)), sem((BLK,)),

time: 79.4 us -> 76.5 us (0.963)
  Pallas kernels: 78.6 us -> 75.7 us
    pallas_call x1, Pallas kernels: 76.8 us -> 73.9 us  [local(): pl.pallas_call(body, out_shape=outs, in_specs=[pl.BlockSpec(memory_space=...]
where the time goes in v4:
time: 76.5 us; the launch traced here: 76.4 us
  Pallas kernels  75.7 us (99%)
    pallas_call x1, Pallas kernels, local(): pl.pallas_call(body, out_shape=outs, in_specs=[pl.BlockSpec(memory_space=...  73.9 us
    pallas_call x1, Pallas kernels, local(): pl.pallas_call(copy_body, out_shape=outs, in_specs=[vspec] * 3, out_specs...  1.81 us

profile of v4, /device:TPU:1, one launch (start us, length us, event | category | flops | bytes accessed | tf_op | source)
XLA Modules:
  0.0 76.4 jit_solution(17960307906242145028)
XLA Ops:
  0.6 73.9 %layer_backward.1 = (bf16[3,128,512]{2,1,0:T(8,128)(2,1)}, f32[8,1536]{1,0:T(8,128)}, f32[8,512]{1,0:T(8,128)}) custom-call(s32[3,3]{1,0:T(4,128)} %nbr.1, bf16[3,128,512]{2,1,0:T(8,128)(2,1)} %bitcast.9, bf16[3,128,512]{2,1,0:T(8,128)(2,1)} %bitcast.10, bf16[512,1536]{1,0:T(8,128)(2,1)} %bitcast.7, bf16[512,512]{1,0:T(8,128)(2,1)} %bitcast.8), custom_call_target="tpu_custom_call" | custom-call | tf_op jit(solution)/shard_map/layer_backward/pallas_call | solution.py:479
  74.6 1.8 %results.1 = (bf16[3,128,512]{2,1,0:T(8,128)(2,1)}, f32[8,1536]{1,0:T(8,128)}, f32[8,512]{1,0:T(8,128)}) custom-call(bf16[3,128,512]{2,1,0:T(8,128)(2,1)} %get-tuple-element.9.a, f32[8,1536]{1,0:T(8,128)} %get-tuple-element.10.b, f32[8,512]{1,0:T(8,128)} %get-tuple-element.11.c), custom_call_target="tpu_custom_call" | custom-call | tf_op jit(solution)/shard_map/results/pallas_call | solution.py:521

commit v5 on v4

--- a/solution.py
+++ b/solution.py
@@ -157,9 +157,6 @@
     forward(1)
     for e in range(1, 4):
         flip(e, 0)
-    halo(kv, 0).wait_recv()
-    flip(0, 0)
-    forward(0)
     load_wo.wait()
 
     def prepare():
@@ -185,8 +182,14 @@
                         o[:, s].reshape(HDIM, TILE).astype(BF)
                     )
 
+    def forward_first():
+        halo(kv, 0).wait_recv()
+        flip(0, 0)
+        forward(0)
+
     @pl.when(sec < SEC - 1)
     def _():
+        forward_first()
         forward_last()
         prepare()
 
@@ -211,7 +214,7 @@
         def _():
             g_copy(b).wait_recv()
 
-    def step(b):
+    def step(b, seen):
         da = dot(g_v[b], wo[...], 1, 1).astype(BF).astype(F32)
         for p in range(PAIRS):
             db = da[:, p * TILE : (p + 1) * TILE]
@@ -223,10 +226,10 @@
             for n, t in enumerate(slots):
                 rows = slice((b + t) * TILE, (b + t + 1) * TILE)
                 val = term[n * TILE : (n + 1) * TILE]
-                if b == 0 or t == 2:
+                if b + t in seen:
+                    acc[rows, cols] = acc[rows, cols] + val
+                else:
                     acc[rows, cols] = val
-                else:
-                    acc[rows, cols] = acc[rows, cols] + val
 
         edge, rest = {0: ((0,), (1, 2)), 1: ((), (0, 1, 2)), 2: ((2,), (0, 1))}[b]
         at = slice(0, 0) if b == 1 else slice(edge[0] * TILE, (edge[0] + 1) * TILE)
@@ -313,40 +316,45 @@
             return dot(xnT[who, :, TILE : TILE + ROWS], dqkv[:, 0:D], 1, 0)
         return dot(xnT[who], accb[:, off - D : off - D + width], 1, 0)
 
+    def sizes(j):
+        return (NY, NZ, y, z) if CHUNKS[j][2] == "y" else (NZ, NY, z, y)
+
+    def by_first(j, val):
+        n1, n2, _, _ = sizes(j)
+        width = CHUNKS[j][1]
+        if CHUNKS[j][2] == "y":
+            return val.reshape(n1, n2 * 8, width)
+        val = val.reshape(NY, NZ, 8, width)
+        return jnp.concatenate([val[i : i + 1] for i in range(NY)], axis=2).reshape(
+            n1, n2 * 8, width
+        )
+
     def open_sum(j):
-        cores[j][0][...] = multiply(j, 1 - c).astype(BF)
+        cores[j][0][...] = by_first(j, multiply(j, 1 - c)).astype(BF)
         c_copy(j).start()
-        cores[j][2][...] = multiply(j, c).reshape(NY, NZ, 8, CHUNKS[j][1])
+
+    def own_half(j):
+        cores[j][2][...] = by_first(j, multiply(j, c))
 
     def first_sum(j):
-        width = CHUNKS[j][1]
+        n1, _, me, _ = sizes(j)
         c_copy(j).wait_recv()
-        held = cores[j][2]
-        held[...] = held[...] + cores[j][1][...].astype(F32).reshape(NY, NZ, 8, width)
-        send = firsts[j][0]
-        if CHUNKS[j][2] == "y":
-            for o in range(1, NY):
-                send[o - 1] = held[lax.rem(y + o, NY)].reshape(NZ * 8, width).astype(BF)
-                axis_copy(j, 0, o).start()
-        else:
-            for o in range(1, NZ):
-                send[o - 1] = held[:, lax.rem(z + o, NZ)].reshape(NY * 8, width).astype(BF)
-                axis_copy(j, 0, o).start()
+        for o in sorted(range(1, n1), key=lambda o: abs(o - n1 // 2)):
+            to = lax.rem(me + o, n1)
+            firsts[j][0][o - 1] = (cores[j][2][to] + cores[j][1][to].astype(F32)).astype(BF)
+            axis_copy(j, 0, o).start()
 
     def fold(piece):
         width = piece.shape[1] // 2
         return jnp.concatenate([piece[:, 0:width], piece[:, width:]], axis=0)
 
     def second_sum(j):
-        width = CHUNKS[j][1]
-        held = cores[j][2]
-        if CHUNKS[j][2] == "y":
-            mine, n1, n2, me = held[y], NY, NZ, z
-        else:
-            mine, n1, n2, me = held[:, z], NZ, NY, y
+        n1, n2, me1, me = sizes(j)
+        mine = cores[j][2][me1] + cores[j][1][me1].astype(F32)
         for o in range(1, n1):
             axis_copy(j, 0, o).wait_recv()
-            mine = mine + firsts[j][1][o - 1].astype(F32).reshape(n2, 8, width)
+            mine = mine + firsts[j][1][o - 1].astype(F32)
+        mine = mine.reshape(n2, 8, CHUNKS[j][1])
         part = firsts[j][2]
         part[...] = mine
         for o in range(1, n2):
@@ -354,8 +362,8 @@
             axis_copy(j, 1, o).start()
 
     def end_sum(j):
-        off, width, first = CHUNKS[j]
-        me, n2 = (z, NZ) if first == "y" else (y, NY)
+        off, width, _ = CHUNKS[j]
+        _, n2, _, me = sizes(j)
         total = fold(firsts[j][2][me])
         for o in range(1, n2):
             axis_copy(j, 1, o).wait_recv()
@@ -366,10 +374,20 @@
         else:
             dwq_ref[:, off : off + width] = total
 
-    wait_g(0)
-    step(0)
-    wait_g(1)
-    step(1)
+    @pl.when(sec < SEC - 1)
+    def _():
+        wait_g(0)
+        step(0, ())
+        wait_g(1)
+        step(1, (1, 2))
+
+    @pl.when(sec == SEC - 1)
+    def _():
+        wait_g(1)
+        step(1, ())
+        forward_first()
+        wait_g(0)
+        step(0, (1, 2))
 
     @pl.when(sec > 0)
     def _():
@@ -383,12 +401,13 @@
     def _():
         wait_g(2)
         open_sum(0)
+        own_half(0)
 
     @pl.when(sec > 0)
     def _():
         wait_g(2)
 
-    step(2)
+    step(2, (2, 3))
 
     @pl.when(sec > 0)
     def _():
@@ -400,13 +419,17 @@
             prepare()
 
         open_sum(0)
-
-    for h in (2, 3, 0, 1):
-        cols = slice(h * (D // 2), (h + 1) * (D // 2))
-        accb[:, cols] = acc[:, cols].astype(BF)
+        own_half(0)
+
+    first_sum(0)
     for j in range(1, len(CHUNKS)):
+        off, width, _ = CHUNKS[j]
+        if off > 0:
+            accb[:, off - D : off - D + width] = acc[:, off - D : off - D + width].astype(BF)
         open_sum(j)
-    for j in range(len(CHUNKS)):
+    for j in range(1, len(CHUNKS)):
+        own_half(j)
+    for j in range(1, len(CHUNKS)):
         first_sum(j)
 
     @pl.when(sec == 0)
@@ -442,10 +465,22 @@
         store(b).wait()
 
 
-def copy_body(a, b, c, a_out, b_out, c_out):
-    a_out[...] = a[...]
-    b_out[...] = b[...]
-    c_out[...] = c[...]
+def copy_body(a, b, c, a_out, b_out, c_out, a_v, b_v, c_v, in_sem, out_sem):
+    parts = [(a.at[i], a_v.at[i], a_out.at[i]) for i in range(BLK)]
+    parts += [(b, b_v, b_out), (c, c_v, c_out)]
+    loads = [
+        pltpu.make_async_copy(src, mid, in_sem.at[i]) for i, (src, mid, _) in enumerate(parts)
+    ]
+    stores = [
+        pltpu.make_async_copy(mid, dst, out_sem.at[i]) for i, (_, mid, dst) in enumerate(parts)
+    ]
+    for load in loads:
+        load.start()
+    for load, store in zip(loads, stores):
+        load.wait()
+        store.start()
+    for store in stores:
+        store.wait()
 
 
 def local(layer_inputs, top_grad, w_qkv, w_out, neighbours):
@@ -462,7 +497,7 @@
     for _, width, first in CHUNKS:
         n1, n2 = (NY, NZ) if first == "y" else (NZ, NY)
         cores.append(
-            (vm((HALF, width), BF), vm((HALF, width), BF), vm((NY, NZ, 8, width), F32), sem(()), sem(()))
+            (vm((n1, n2 * 8, width), BF), vm((n1, n2 * 8, width), BF), vm((n1, n2 * 8, width), F32), sem(()), sem(()))
         )
         firsts.append(
             (
@@ -521,8 +556,10 @@
     gin, dwq, dwo = pl.pallas_call(
         copy_body,
         out_shape=outs,
-        in_specs=[vspec] * 3,
-        out_specs=(vspec,) * 3,
+        in_specs=[anyspec] * 3,
+        out_specs=(anyspec,) * 3,
+        scratch_shapes=[vm(o.shape, o.dtype) for o in outs]
+        + [sem((BLK + 2,)), sem((BLK + 2,))],
         name="results",
     )(*results)
     return (gin.reshape(1, 1, ROWS, D), dwq[None], dwo[None])

time: 76.5 us -> 75.3 us (0.984)
  Pallas kernels: 75.7 us -> 74.2 us
    pallas_call x1, Pallas kernels: 73.9 us -> 72.4 us  [local(): pl.pallas_call(body, out_shape=outs, in_specs=[pl.BlockSpec(memory_space=...]
where the time goes in v5:
time: 75.3 us; the launch traced here: 75 us
  Pallas kernels  74.2 us (99%)
  between operations  0.8 us (1%)
    pallas_call x1, Pallas kernels, local(): pl.pallas_call(body, out_shape=outs, in_specs=[pl.BlockSpec(memory_space=...  72.4 us
    pallas_call x1, Pallas kernels, local(): pl.pallas_call(copy_body, out_shape=outs, in_specs=[anyspec] * 3, out_spe...  1.78 us

profile of v5, /device:TPU:1, one launch (start us, length us, event | category | flops | bytes accessed | tf_op | source)
XLA Modules:
  0.0 75.0 jit_solution(8422266125708343765)
XLA Ops:
  0.6 72.4 %layer_backward.1 = (bf16[3,128,512]{2,1,0:T(8,128)(2,1)}, f32[8,1536]{1,0:T(8,128)}, f32[8,512]{1,0:T(8,128)}) custom-call(s32[3,3]{1,0:T(4,128)} %nbr.1, bf16[3,128,512]{2,1,0:T(8,128)(2,1)} %bitcast.9, bf16[3,128,512]{2,1,0:T(8,128)(2,1)} %bitcast.10, bf16[512,1536]{1,0:T(8,128)(2,1)} %bitcast.7, bf16[512,512]{1,0:T(8,128)(2,1)} %bitcast.8), custom_call_target="tpu_custom_call" | custom-call | tf_op jit(solution)/shard_map/layer_backward/pallas_call | solution.py:514
  73.0 1.8 %results.1 = (bf16[3,128,512]{2,1,0:T(8,128)(2,1)}, f32[8,1536]{1,0:T(8,128)}, f32[8,512]{1,0:T(8,128)}) custom-call(bf16[3,128,512]{2,1,0:T(8,128)(2,1)} %get-tuple-element.9.a, f32[8,1536]{1,0:T(8,128)} %get-tuple-element.10.b, f32[8,512]{1,0:T(8,128)} %get-tuple-element.11.c), custom_call_target="tpu_custom_call" | custom-call | tf_op jit(solution)/shard_map/results/pallas_call | solution.py:556

commit v6 on v5

--- a/solution.py
+++ b/solution.py
@@ -160,8 +160,6 @@
     load_wo.wait()
 
     def prepare():
-        halo(xn, 0).wait_recv()
-        halo(xn, 1).wait_recv()
         for e in range(EXT // TILE):
             flip(e, 1)
             cols = slice(e * TILE, (e + 1) * TILE)
@@ -191,6 +189,8 @@
     def _():
         forward_first()
         forward_last()
+        halo(xn, 0).wait_recv()
+        halo(xn, 1).wait_recv()
         prepare()
 
     def g_copy(b):
@@ -213,6 +213,13 @@
         @pl.when(sec < SEC - 1)
         def _():
             g_copy(b).wait_recv()
+
+    def project(dn, xh):
+        return (
+            dn
+            - jnp.mean(dn, axis=-1, keepdims=True)
+            - xh * jnp.mean(dn * xh, axis=-1, keepdims=True)
+        )
 
     def step(b, seen):
         da = dot(g_v[b], wo[...], 1, 1).astype(BF).astype(F32)
@@ -234,13 +241,14 @@
         edge, rest = {0: ((0,), (1, 2)), 1: ((), (0, 1, 2)), 2: ((2,), (0, 1))}[b]
         at = slice(0, 0) if b == 1 else slice(edge[0] * TILE, (edge[0] + 1) * TILE)
         inner = slice(rest[0] * TILE, (rest[-1] + 1) * TILE)
-        side = b // 2
         if b != 1:
             for p in range(PAIRS):
                 term = dot(pr[b * PAIRS + p, at, :], da2[b * PAIRS + p], 1, 0)
                 add(edge, term, D, p)
-                rim_out[side, 1, :, p * TILE : (p + 1) * TILE] = term.astype(BF)
-            rim(side, 1).start()
+                if b == 0:
+                    rim_out[0, 1, :, p * TILE : (p + 1) * TILE] = term.astype(BF)
+            if b == 0:
+                rim(0, 1).start()
         for p in range(PAIRS):
             vals = kv[b * TILE : b * TILE + KEYS, D + p * TILE : D + (p + 1) * TILE]
             dp = dot(vals, da2[b * PAIRS + p], 1, 1)
@@ -251,9 +259,16 @@
             if b != 1:
                 term = dot(ds[at], q2[b * PAIRS + p], 1, 0)
                 add(edge, term, 0, p)
-                rim_out[side, 0, :, p * TILE : (p + 1) * TILE] = term.astype(BF)
-        if b != 1:
-            rim(side, 0).start()
+                if b == 0:
+                    rim_out[0, 0, :, p * TILE : (p + 1) * TILE] = term.astype(BF)
+        if b == 0:
+            rim(0, 0).start()
+        if b == 2:
+            far = acc[EXT - TILE :, :].astype(BF)
+            rim_out[1, 0] = project(
+                dot(far, wq[:, D:], 1, 1), xn[EXT - TILE :, :].astype(F32)
+            ).astype(BF)
+            rim(1, 0).start()
         for p in range(PAIRS):
             add(rest, dot(pr[b * PAIRS + p, inner, :], da2[b * PAIRS + p], 1, 0), D, p)
             add(rest, dot(dsc[p, inner, :], q2[b * PAIRS + p], 1, 0), 0, p)
@@ -263,23 +278,20 @@
 
     def close(b):
         dkv = acc[(b + 1) * TILE : (b + 2) * TILE, :]
-        if b != 1:
-            side = b // 2
-            rim(side, 0).wait_recv()
-            rim(side, 1).wait_recv()
-            dkv = dkv + jnp.concatenate([rim_in[side, 0], rim_in[side, 1]], axis=1).astype(F32)
+        if b == 0:
+            rim(0, 0).wait_recv()
+            rim(0, 1).wait_recv()
+            dkv = dkv + jnp.concatenate([rim_in[0, 0], rim_in[0, 1]], axis=1).astype(F32)
         dqkv[b * TILE : (b + 1) * TILE, D:] = dkv.astype(BF)
 
     def finish(b):
         rows = pl.ds(b * TILE, TILE)
         dn = dot(dqkv[rows, :], wq[...], 1, 1)
-        xh = xhat[rows, :]
-        inv = inv_v[rows, 0:1]
-        ln = inv * (
-            dn
-            - jnp.mean(dn, axis=-1, keepdims=True)
-            - xh * jnp.mean(dn * xh, axis=-1, keepdims=True)
-        )
+        part = project(dn, xhat[rows, :])
+        if b == 2:
+            rim(1, 0).wait_recv()
+            part = part + rim_in[1, 0].astype(F32)
+        ln = inv_v[rows, 0:1] * part
         gout[b] = (g_v[b].astype(F32) + ln).astype(BF)
 
     def store(b):
@@ -396,6 +408,8 @@
     @pl.when(sec == SEC - 1)
     def _():
         forward_last()
+        halo(xn, 0).wait_recv()
+        halo(xn, 1).wait_recv()
 
     @pl.when(sec == 0)
     def _():
@@ -448,7 +462,7 @@
         halo(kv, side).wait_send()
         halo(xn, side).wait_send()
         rim(side, 0).wait_send()
-        rim(side, 1).wait_send()
+    rim(0, 1).wait_send()
 
     @pl.when(sec > 0)
     def _():

time: 75.3 us -> 74.8 us (level)
  no operation moved by 1% of the time
where the time goes in v6:
time: 74.8 us; the launch traced here: 74.6 us
  Pallas kernels  73.8 us (99%)
  between operations  0.8 us (1%)
    pallas_call x1, Pallas kernels, local(): pl.pallas_call(body, out_shape=outs, in_specs=[pl.BlockSpec(memory_space=...  72 us
    pallas_call x1, Pallas kernels, local(): pl.pallas_call(copy_body, out_shape=outs, in_specs=[anyspec] * 3, out_spe...  1.78 us

profile of v6, /device:TPU:1, one launch (start us, length us, event | category | flops | bytes accessed | tf_op | source)
XLA Modules:
  0.0 74.6 jit_solution(7788086899014578004)
XLA Ops:
  0.6 72.0 %layer_backward.1 = (bf16[3,128,512]{2,1,0:T(8,128)(2,1)}, f32[8,1536]{1,0:T(8,128)}, f32[8,512]{1,0:T(8,128)}) custom-call(s32[3,3]{1,0:T(4,128)} %nbr.1, bf16[3,128,512]{2,1,0:T(8,128)(2,1)} %bitcast.9, bf16[3,128,512]{2,1,0:T(8,128)(2,1)} %bitcast.10, bf16[512,1536]{1,0:T(8,128)(2,1)} %bitcast.7, bf16[512,512]{1,0:T(8,128)(2,1)} %bitcast.8), custom_call_target="tpu_custom_call" | custom-call | tf_op jit(solution)/shard_map/layer_backward/pallas_call | solution.py:528
  72.7 1.8 %results.1 = (bf16[3,128,512]{2,1,0:T(8,128)(2,1)}, f32[8,1536]{1,0:T(8,128)}, f32[8,512]{1,0:T(8,128)}) custom-call(bf16[3,128,512]{2,1,0:T(8,128)(2,1)} %get-tuple-element.9.a, f32[8,1536]{1,0:T(8,128)} %get-tuple-element.10.b, f32[8,512]{1,0:T(8,128)} %get-tuple-element.11.c), custom_call_target="tpu_custom_call" | custom-call | tf_op jit(solution)/shard_map/results/pallas_call | solution.py:570

commit v7 on v6

--- a/solution.py
+++ b/solution.py
@@ -221,7 +221,14 @@
             - xh * jnp.mean(dn * xh, axis=-1, keepdims=True)
         )
 
-    def step(b, seen):
+    def send_far():
+        far = acc[EXT - TILE :, :].astype(BF)
+        rim_out[1, 0] = project(
+            dot(far, wq[:, D:], 1, 1), xn[EXT - TILE :, :].astype(F32)
+        ).astype(BF)
+        rim(1, 0).start()
+
+    def step(b, seen, last=False):
         da = dot(g_v[b], wo[...], 1, 1).astype(BF).astype(F32)
         for p in range(PAIRS):
             db = da[:, p * TILE : (p + 1) * TILE]
@@ -263,12 +270,8 @@
                     rim_out[0, 0, :, p * TILE : (p + 1) * TILE] = term.astype(BF)
         if b == 0:
             rim(0, 0).start()
-        if b == 2:
-            far = acc[EXT - TILE :, :].astype(BF)
-            rim_out[1, 0] = project(
-                dot(far, wq[:, D:], 1, 1), xn[EXT - TILE :, :].astype(F32)
-            ).astype(BF)
-            rim(1, 0).start()
+        if b == 2 and not last:
+            send_far()
         for p in range(PAIRS):
             add(rest, dot(pr[b * PAIRS + p, inner, :], da2[b * PAIRS + p], 1, 0), D, p)
             add(rest, dot(dsc[p, inner, :], q2[b * PAIRS + p], 1, 0), 0, p)
@@ -416,12 +419,12 @@
         wait_g(2)
         open_sum(0)
         own_half(0)
+        step(2, (2, 3), True)
 
     @pl.when(sec > 0)
     def _():
         wait_g(2)
-
-    step(2, (2, 3))
+        step(2, (2, 3))
 
     @pl.when(sec > 0)
     def _():
@@ -441,6 +444,11 @@
         if off > 0:
             accb[:, off - D : off - D + width] = acc[:, off - D : off - D + width].astype(BF)
         open_sum(j)
+
+    @pl.when(sec == 0)
+    def _():
+        send_far()
+
     for j in range(1, len(CHUNKS)):
         own_half(j)
     for j in range(1, len(CHUNKS)):

time: 74.8 us -> 74.2 us (level)
  Pallas kernels: 73.8 us -> 72.9 us
    pallas_call x1, Pallas kernels: 72 us -> 71.1 us  [local(): pl.pallas_call(body, out_shape=outs, in_specs=[pl.BlockSpec(memory_space=...]
where the time goes in v7:
time: 74.2 us; the launch traced here: 73.7 us
  Pallas kernels  72.9 us (98%)
  between operations  0.8 us (1%)
    pallas_call x1, Pallas kernels, local(): pl.pallas_call(body, out_shape=outs, in_specs=[pl.BlockSpec(memory_space=...  71.1 us
    pallas_call x1, Pallas kernels, local(): pl.pallas_call(copy_body, out_shape=outs, in_specs=[anyspec] * 3, out_spe...  1.78 us

profile of v7, /device:TPU:1, one launch (start us, length us, event | category | flops | bytes accessed | tf_op | source)
XLA Modules:
  0.0 73.7 jit_solution(11895114448588926498)
XLA Ops:
  0.6 71.1 %layer_backward.1 = (bf16[3,128,512]{2,1,0:T(8,128)(2,1)}, f32[8,1536]{1,0:T(8,128)}, f32[8,512]{1,0:T(8,128)}) custom-call(s32[3,3]{1,0:T(4,128)} %nbr.1, bf16[3,128,512]{2,1,0:T(8,128)(2,1)} %bitcast.9, bf16[3,128,512]{2,1,0:T(8,128)(2,1)} %bitcast.10, bf16[512,1536]{1,0:T(8,128)(2,1)} %bitcast.7, bf16[512,512]{1,0:T(8,128)(2,1)} %bitcast.8), custom_call_target="tpu_custom_call" | custom-call | tf_op jit(solution)/shard_map/layer_backward/pallas_call | solution.py:536
  71.8 1.8 %results.1 = (bf16[3,128,512]{2,1,0:T(8,128)(2,1)}, f32[8,1536]{1,0:T(8,128)}, f32[8,512]{1,0:T(8,128)}) custom-call(bf16[3,128,512]{2,1,0:T(8,128)(2,1)} %get-tuple-element.9.a, f32[8,1536]{1,0:T(8,128)} %get-tuple-element.10.b, f32[8,512]{1,0:T(8,128)} %get-tuple-element.11.c), custom_call_target="tpu_custom_call" | custom-call | tf_op jit(solution)/shard_map/results/pallas_call | solution.py:578
